TPU v7x, 512 devices: a whole 4x4x16 slice. The times are simulated.
512 devices in a mesh: col: 64 (over x, z), tm: 8 (over y, core).
Axes of the slice: x: 4, y: 4, z: 16, core: 2. Of those that a mesh axis runs over, the one named last changes fastest.
Arguments:
- series: bfloat16 [1200, 98304], P(None, 'col'), may hold values from -700 to 700
- slab_series: float32 [1200, 2048], P('tm', 'col'), may hold values from -700 to 700
- phase_index: int32 [4, 600], P(None, 'tm'), may hold values from 0 to 1199
Outputs:
- tile_peak: float32 [4, 2048, 64], P(None, None, 'col')
- peak_all: float32 [4], replicated
All inputs are finite; a program needn't handle non-finite values.
Results may differ from a plain program's by a relative error of at most 0.0013.
Values may be sent and summed in bfloat16 or wider, within the bound.
A program may use at most 64 MiB of HBM per device.

v0:
```python
import functools
import math

import jax
import jax.numpy as jnp
from jax import lax
from jax.sharding import Mesh
from jax.sharding import PartitionSpec as P

FRAMES = 1200
FREQS = 600
COL = ("col_0", "col_1")


EPSILON = 1e-06
HIGHEST = lax.Precision.HIGHEST


def laid_out(parts, dim):
    shape = list(parts.shape[1:])
    shape[dim] *= parts.shape[0]
    return jnp.moveaxis(parts, 0, dim).reshape(shape)


def sent_to_all(value, axis):
    copies = jnp.broadcast_to(value, (lax.axis_size(axis), *value.shape))
    return lax.all_to_all(copies, axis, split_axis=0, concat_axis=0, tiled=True)


def gathered_copies(value, axis, dim):
    return laid_out(sent_to_all(value, axis), dim)


def all_blocks(value, axes, sequence):
    parts = value[None]
    for k in sequence:
        parts = lax.all_gather(parts, axes[k], axis=0, tiled=True)
    current = [lax.axis_size(axes[k]) for k in reversed(sequence)]
    parts = parts.reshape(*current, *value.shape)
    turned = sorted(range(len(sequence)), key=lambda place: sequence[len(sequence) - 1 - place])
    return parts.transpose(*turned, *range(len(sequence), parts.ndim)).reshape(-1, *value.shape)


def gathered_by_axis(value, axes, sequence, dim):
    return laid_out(all_blocks(value, axes, sequence), dim)


def by_axis(value, axes):
    return functools.reduce(lax.pmax, axes, value)


def twiddle(frame_ids, freq_ids):
    turn_count = frame_ids[:, None] * freq_ids[None, :] % FRAMES
    angles = turn_count.astype(jnp.float32) * (2.0 * math.pi / FRAMES)
    return (jnp.cos(angles), jnp.sin(angles))


def rotate_back(spec_cos, spec_sin, phase_ids, freq_ids, cos_back, sin_back):
    phase_angle = phase_ids.astype(jnp.float32) * (2.0 * math.pi / FRAMES)
    phase_cos = jnp.cos(phase_angle)[:, :, None]
    phase_sin = jnp.sin(phase_angle)[:, :, None]
    weights = (jnp.where(freq_ids < FREQS, 2.0, 1.0) / FRAMES).astype(jnp.float32)[None, :, None]
    rot_real = (spec_cos[None] * phase_cos + spec_sin[None] * phase_sin) * weights
    rot_imag = (spec_cos[None] * phase_sin - spec_sin[None] * phase_cos) * weights
    return jnp.einsum("sfv,tf->svt", rot_real, cos_back, precision=HIGHEST) - jnp.einsum(
        "sfv,tf->svt", rot_imag, sin_back, precision=HIGHEST
    )


def normalize_rows(surrogate):
    return (
        surrogate * lax.rsqrt(jnp.sum(surrogate * surrogate, axis=2, keepdims=True) + EPSILON)
    ).astype(jnp.bfloat16)


def peak_update(normed_rows, normed_cols):
    scores = jnp.einsum("srt,tc->src", normed_rows, normed_cols, preferred_element_type=jnp.float32)
    row_top = jnp.max(jnp.abs(scores), axis=2)
    return row_top


def body(series, slab_series, phase_index):
    values = series.astype(jnp.float32)
    centered = values - jnp.mean(values, axis=0, keepdims=True)
    normed_cols = (
        centered * lax.rsqrt(jnp.sum(centered * centered, axis=0, keepdims=True) + EPSILON)
    ).astype(jnp.bfloat16)
    surr_count = phase_index.shape[0]
    n_col = lax.axis_size(COL)
    n_tm = lax.axis_size("tm")
    row_share = slab_series.shape[1] // n_tm
    own_frames = lax.all_to_all(slab_series, "tm", split_axis=1, concat_axis=0, tiled=True)
    own_phase = gathered_copies(phase_index, "tm", 1)
    every_freq = jnp.arange(1, FREQS + 1, dtype=jnp.int32)
    cos_every, sin_every = twiddle(jnp.arange(FRAMES, dtype=jnp.int32), every_freq)
    own_cos = jnp.dot(cos_every.T, own_frames, precision=HIGHEST)
    own_sin = jnp.dot(sin_every.T, own_frames, precision=HIGHEST)
    own_normed = normalize_rows(
        rotate_back(own_cos, own_sin, own_phase, every_freq, cos_every, sin_every)
    )
    running = peak_update(gathered_by_axis(own_normed, COL, (0, 1), 1), normed_cols)
    scaled = running * math.sqrt(FRAMES)
    gathered = gathered_copies(scaled.reshape(surr_count, n_col, 1, row_share), "tm", 2)
    full_peaks = gathered.reshape(surr_count, n_col * n_tm * row_share)
    peak_all = by_axis(jnp.max(full_peaks, axis=1), COL)
    return (full_peaks[:, :, None], peak_all)


def solution(mesh):
    finer = Mesh(mesh.devices.reshape(4, 16, mesh.shape["tm"]), ("col_0", "col_1", "tm"))
    placed = (P(None, COL), P("tm", COL), P(None, "tm"))
    return jax.shard_map(
        body, mesh=finer, in_specs=placed, out_specs=(P(None, None, COL), P()), check_vma=False
    )
```

profile of v0, /device:TPU:8, one launch (start us, length us, event | category | flops | bytes accessed | tf_op | source)
XLA Modules:
  0.0 242.8 jit_solution(10669539949304442477)
XLA Ops:
  7.2 1.3 broadcast_in_dim.14
  8.4 9.0 %all-to-all-start.1 = ((s32[8,4,75]{2,1,0:T(4,128)}), s32[8,4,75]{2,1,0:T(4,128)S(1)}, u32[]{:S(2)}, u32[]{:S(2)}) async-start(s32[8,4,75]{2,1,0:T(4,128)} %broadcast_in_dim.14), calls=%async_computation.1 | async-start | bytes 32768 | tf_op jit(solution)/shard_map/all_to_all | solution.py:27
  17.5 1.4 all_to_all.20
  18.9 2.5 %all-to-all-done.1 = s32[8,4,75]{2,1,0:T(4,128)S(1)} async-done(((s32[8,4,75]{2,1,0:T(4,128)}), s32[8,4,75]{2,1,0:T(4,128)S(1)}, u32[]{:S(2)}, u32[]{:S(2)}) %all-to-all-start.1) | async-done | bytes 9632 | tf_op jit(solution)/shard_map/all_to_all | solution.py:27
  21.4 4.7 %all-to-all-start = ((f32[150,8,4]{0,2,1:T(4,128)}), f32[150,8,4]{0,2,1:T(4,128)S(1)}, u32[]{:S(2)}, u32[]{:S(2)}) async-start(f32[150,8,4]{0,2,1:T(4,128)} %all_to_all.20), calls=%async_computation | async-start | bytes 65536 | tf_op jit(solution)/shard_map/all_to_all | solution.py:92
  26.1 0.1 cosine_bitcast_fusion
  26.4 3.7 %all-to-all-done = f32[150,8,4]{0,2,1:T(4,128)S(1)} async-done(((f32[150,8,4]{0,2,1:T(4,128)}), f32[150,8,4]{0,2,1:T(4,128)S(1)}, u32[]{:S(2)}, u32[]{:S(2)}) %all-to-all-start) | async-done | bytes 19232 | tf_op jit(solution)/shard_map/all_to_all | solution.py:92
  30.1 0.1 all_to_all.23
  30.2 14.0 %fusion.19 = f32[600,4]{0,1:T(4,128)S(1)} fusion(f32[1200,4]{0,1:T(4,128)S(1)} %all_to_all.23, s32[600]{0:T(1024)S(1)} %iota_add_fusion), kind=kOutput, calls=%fused_computation.22 | convolution fusion | flops 41040000 | bytes 31200 | tf_op jit(solution)/shard_map/dot_general | solution.py:96
  44.2 14.1 %fusion.22 = f32[600,4]{0,1:T(4,128)S(1)} fusion(f32[1200,4]{0,1:T(4,128)S(1)} %all_to_all.23, s32[600]{0:T(1024)S(1)} %iota_add_fusion), kind=kOutput, calls=%fused_computation.23 | convolution fusion | flops 41040000 | bytes 31200 | tf_op jit(solution)/shard_map/dot_general | solution.py:97
  58.3 15.3 %fusion.10 = f32[4,4,1200]{2,1,0:T(4,128)S(1)} fusion(s32[600]{0:T(1024)S(1)} %iota_add_fusion, f32[600]{0:T(1024)S(1)} %select_multiply_fusion, f32[4,600]{1,0:T(4,128)S(1)} %sin.21, f32[600,4]{0,1:T(4,128)S(1)} %fusion.22, f32[4,600]{1,0:T(4,128)S(1)} %cos.21, f32[600,4]{0,1:T(4,128)S(1)} %fusion.19), kind=kOutput, calls=%fused_computation.13 | convolution fusion | flops 144758400 | bytes 120000 | tf_op jit(solution)/shard_map/sfv,tf->svt/dot_general | solution.py:65
  73.6 15.3 %multiply_reduce_fusion = (f32[4,4]{1,0:T(4,128)S(1)}, f32[4,4,1200]{2,1,0:T(4,128)S(1)}) fusion(f32[4,4,1200]{2,1,0:T(4,128)S(1)} %fusion.10, s32[600]{0:T(1024)S(1)} %iota_add_fusion, f32[600]{0:T(1024)S(1)} %select_multiply_fusion, f32[4,600]{1,0:T(4,128)S(1)} %sin.21, f32[600,4]{0,1:T(4,128)S(1)} %fusion.22, f32[4,600]{1,0:T(4,128)S(1)} %cos.21, ...), kind=kOutput, calls=%fused_computation.40 | convolution fusion | flops 144815984 | bytes 196864 | tf_op jit(solution)/shard_map/sfv,tf->svt/dot_general | solution.py:65
  88.9 0.1 multiply_convert_fusion
  89.0 13.1 %all-gather = bf16[16,4,1200]{2,1,0:T(4,128)(2,1)} all-gather(bf16[4,4,1200]{2,1,0:T(4,128)(2,1)S(1)} %multiply_convert_fusion), channel_id=2, replica_groups=mesh['col_0'=4,'col_1'=16,'tm'=8] {'col_0'}, dimensions={0}, use_global_device_ids=true | all-gather | bytes 192000 | tf_op jit(solution)/shard_map/all_gather | solution.py:37
  102.1 2.8 %convert_reduce_fusion = f32[1536]{0:T(1024)S(1)} fusion(bf16[1200,1536]{1,0:T(8,128)(2,1)} %param.3), kind=kLoop, calls=%fused_computation.1 | loop fusion | flops 3684864 | bytes 3692544 | tf_op jit(solution)/shard_map/reduce_sum | solution.py:84
  104.9 0.4 copy-done
  105.2 1.0 fusion.2
  106.3 69.0 %all-gather.3.cloned.1.call-done = bf16[64,4,4,1200]{3,2,1,0:T(4,128)(2,1)} async-done(((bf16[4,4,4,1200]{3,2,1,0:T(4,128)(2,1)}), bf16[64,4,4,1200]{3,2,1,0:T(4,128)(2,1)}) %all-gather.3.cloned.1.call-update) | async-done | bytes 2457616 | tf_op jit(solution)/shard_map/all_gather | solution.py:37
  175.3 3.0 %copy.19 = bf16[4,16,4,4,1200]{4,2,3,1,0:T(4,128)(2,1)S(1)} copy(bf16[4,16,4,4,1200]{4,3,2,0,1:T(4,128)(2,1)} %bitcast.44) | data formatting | bytes 4915200 | tf_op jit(solution)/shard_map/transpose | solution.py:41
  178.2 4.7 %abs_reduce_fusion = f32[4,256]{1,0:T(4,128)S(1)} fusion(bf16[1200,1536]{1,0:T(8,128)(2,1)S(1)} %copy-done.1, f32[1536]{0:T(1024)S(1)} %add_rsqrt_fusion, f32[1536]{0:T(1024)S(1)} %broadcast_multiply_fusion, bf16[4,256,1200]{2,0,1:T(4,128)(2,1)S(1)} %bitcast.45), kind=kOutput, calls=%fused_computation.6 | convolution fusion | flops 3785391104 | bytes 6160384 | tf_op jit(solution)/shard_map/srt,tc->src/dot_general | solution.py:77
  182.9 0.1 mul.177
  183.1 0.1 copy.21
  183.2 0.1 reshape.75
  183.3 8.6 %all_to_all.29 = f32[8,1,1024]{2,1,0:T(1,128)S(1)} all-to-all(f32[8,1,1024]{2,1,0:T(1,128)S(1)} %reshape.75), channel_id=1, replica_groups=mesh['col_0'=4,'col_1'=16,'tm'=8] {'tm'}, dimensions={0} | all-to-all | bytes 65536 | tf_op jit(solution)/shard_map/all_to_all | solution.py:27
  191.9 0.5 broadcast.66
  192.4 0.7 reduce.2
  193.2 0.1 reshape.76
  193.3 0.1 bitcast_reduce_fusion
  193.4 0.4 copy.22
  193.9 10.4 %pmax.14 = f32[4]{0:T(128)S(1)} all-reduce(f32[4]{0:T(128)S(1)} %bitcast_reduce_fusion), channel_id=1, replica_groups=mesh['col_0'=4,'col_1'=16,'tm'=8] {'col_0'}, use_global_device_ids=true, to_apply=%region_5.6 | all-reduce | flops 4 | bytes 32 | tf_op jit(solution)/shard_map/pmax | solution.py:49
  204.3 1.4 broadcast_in_dim_reshape_reshape.4
  205.6 30.3 %pmax.15 = f32[4]{0:T(128)} all-reduce(f32[4]{0:T(128)S(1)} %pmax.14), channel_id=1, replica_groups=mesh['col_0'=4,'col_1'=16,'tm'=8] {'col_1'}, use_global_device_ids=true, to_apply=%region_6.7 | all-reduce | flops 4 | bytes 32 | tf_op jit(solution)/shard_map/pmax | solution.py:49
  (18 shorter events, 0.3 us)
Async XLA Ops:
  8.4 13.0 %all-to-all-start.1 = ((s32[8,4,75]{2,1,0:T(4,128)}), s32[8,4,75]{2,1,0:T(4,128)S(1)}, u32[]{:S(2)}, u32[]{:S(2)}) async-start(s32[8,4,75]{2,1,0:T(4,128)} %broadcast_in_dim.14), calls=%async_computation.1 | async-start | bytes 32768 | tf_op jit(solution)/shard_map/all_to_all | solution.py:27
  21.4 8.7 %all-to-all-start = ((f32[150,8,4]{0,2,1:T(4,128)}), f32[150,8,4]{0,2,1:T(4,128)S(1)}, u32[]{:S(2)}, u32[]{:S(2)}) async-start(f32[150,8,4]{0,2,1:T(4,128)} %all_to_all.20), calls=%async_computation | async-start | bytes 65536 | tf_op jit(solution)/shard_map/all_to_all | solution.py:92
  26.1 149.2 %all-gather.3.cloned.1.call-start = ((), (), s32[]{:S(2)}) async-start(), calls=%async_computation.3 | async-start | bytes 2785280 | tf_op jit(solution)/shard_map/all_gather | solution.py:37
  102.1 3.2 %copy-start = (bf16[1200,1536]{1,0:T(8,128)(2,1)S(1)}, bf16[1200,1536]{1,0:T(8,128)(2,1)}, u32[]{:S(2)}) copy-start(bf16[1200,1536]{1,0:T(8,128)(2,1)} %param.3) | copy-start | bytes 11059204
  175.3 3.0 %copy-start.1 = (bf16[1200,1536]{1,0:T(8,128)(2,1)S(1)}, bf16[1200,1536]{1,0:T(8,128)(2,1)}, u32[]{:S(2)}) copy-start(bf16[1200,1536]{1,0:T(8,128)(2,1)} %param.3) | copy-start | bytes 11059204
Sparse Core Ops, SparseCore 0:
  102.2 73.0 all-gather.2
where the time goes:
time: 243 us
  waiting for transfers between devices  75.2 us (31%)
  matrix products  63.3 us (26%)
  blocking collectives  62.4 us (26%)
  between operations  14.2 us (6%)
  starting transfers between devices  13.7 us (6%)
  local copies, waits for them, and re-layouts  9.04 us (4%)
  other arithmetic  4.89 us (2%)
    all_gather x1, waiting for transfers between devices, all_blocks(): parts = lax.all_gather(parts, axes[k], axis=0, tiled=True)  69 us
    pmax x2, blocking collectives, by_axis(): return functools.reduce(lax.pmax, axes, value)  40.8 us
    dot_general x1, matrix products, rotate_back(): jnp.einsum('sfv,tf->svt', rot_real, cos_back, precision=HIGHEST)  15.3 us
    dot_general x1, matrix products, rotate_back(): jnp.einsum('sfv,tf->svt', rot_imag, sin_back, precision=HIGHEST)  15.3 us
    dot_general x1, matrix products, body(): own_sin = jnp.dot(sin_every.T, own_frames, precision=HIGHEST)  14.1 us
    dot_general x1, matrix products, body(): own_cos = jnp.dot(cos_every.T, own_frames, precision=HIGHEST)  14 us
    all_gather x1, blocking collectives, all_blocks(): parts = lax.all_gather(parts, axes[k], axis=0, tiled=True)  13.1 us
    all_to_all x1, starting transfers between devices, sent_to_all(): return lax.all_to_all(copies, axis, split_axis=0, concat_axis=0, tiled=True)  9.04 us
  transfers between devices with their start and end apart: 3, of which 3 were waited for; matrix products, arithmetic and copies ran while one was open for 2% of the time, Pallas kernels for 0%

commit v1 on v0

v1 whole, which is shorter than its diff:
```python
import functools
import math

import jax
import jax.numpy as jnp
import numpy as np
from jax import lax
from jax.experimental import pallas as pl
from jax.experimental.pallas import tpu as pltpu
from jax.sharding import PartitionSpec as P

FRAMES = 1200
FREQS = 600
FP = 640
TP = 1280
SURR = 4
COLS = 1536
EPS = 1e-6
F32 = jnp.float32
BF16 = jnp.bfloat16
MESH = pl.DeviceIdType.MESH
NEAR = (4, -4, 3, -3, 2, -2, 1, -1)


def basis_tables():
    freq = np.arange(1, FP + 1)[:, None]
    lane = np.arange(128)[None, :]
    fine = 2.0 * np.pi * ((freq * lane) % FRAMES) / FRAMES
    step = np.broadcast_to(2.0 * np.pi * ((freq * 128) % FRAMES) / FRAMES, fine.shape)
    return np.stack([np.cos(fine), np.sin(fine), np.cos(step), np.sin(step)]).astype(np.float32)


def dot(a, b):
    return lax.dot_general(a, b, (((1,), (0,)), ((), ())), preferred_element_type=F32)


def dot_t(a, b):
    return lax.dot_general(a, b, (((1,), (1,)), ((), ())), preferred_element_type=F32)


def kernel(
    series, slab, phase, basis, out_tile, out_peak,
    cols, bas, thi, tlo, kc, held, chunks, angles, spec, rot, best, mine, parts, own_top, top1, wide_top, top2, line_top, top3,
    col_sem, bas_sem, chunk_send, chunk_recv, ang_send, ang_recv, near_send, relay_send, x_send, unit_recv,
    part_send, part_recv, t1_send, t1_recv, t2_send, t2_recv, t3_send, t3_recv,
):
    col = lax.axis_index("col")
    k = lax.axis_index("tm")
    xx = lax.div(col, 16)
    z = lax.rem(col, 16)
    residue = lax.rem(k, 4)
    half = lax.div(k, 4)
    z_low = lax.rem(z, 4)
    hub = z_low == residue

    def at_z(d):
        return (xx * 16 + lax.rem(z + d + 16, 16), k)

    def at_x(d):
        return (lax.rem(xx + d, 4) * 16 + z, k)

    def at_k(d):
        return (col, lax.rem(k + d, 8))

    def remote(src, dst, send, recv, dev):
        return pltpu.make_async_remote_copy(
            src_ref=src, dst_ref=dst, send_sem=send, recv_sem=recv, device_id=dev, device_id_type=MESH
        )

    series_copy = pltpu.make_async_copy(series, cols.at[pl.ds(0, FRAMES)], col_sem)
    basis_copy = pltpu.make_async_copy(basis, bas, bas_sem)
    basis_copy.start()
    series_copy.start()

    barrier = pltpu.get_barrier_semaphore()
    peers = [at_k(d) for d in range(1, 8)] + [at_x(d) for d in range(1, 4)] + [at_z(d) for d in NEAR]
    for dev in peers:
        pl.semaphore_signal(barrier, inc=1, device_id=dev, device_id_type=MESH)

    cols[pl.ds(FRAMES, TP - FRAMES), :] = jnp.zeros((TP - FRAMES, COLS), BF16)
    basis_copy.wait()

    def make_rows(i, _):
        at = pl.multiple_of(i * 64, 64)
        c = bas[0, pl.ds(at, 64), :]
        s = bas[1, pl.ds(at, 64), :]
        sc = bas[2, pl.ds(at, 64), :]
        ss = bas[3, pl.ds(at, 64), :]
        for a in range(10):
            lanes = pl.ds(a * 128, 128)
            for base, val in ((0, c), (FP, s)):
                hi = val.astype(BF16)
                thi[pl.ds(base + at, 64), lanes] = hi
                tlo[pl.ds(base + at, 64), lanes] = (val - hi.astype(F32)).astype(BF16)
            c, s = c * sc - s * ss, s * sc + c * ss
        return 0

    lax.fori_loop(0, 10, make_rows, 0)

    pl.semaphore_wait(barrier, 18)

    for h in range(2):
        target = h * 4 + z_low

        @pl.when(target != k)
        def _():
            remote(slab.at[pl.ds(h * 16, 16)], chunks.at[k], chunk_send.at[h], chunk_recv.at[k], (col, target)).start()

    for d in range(1, 8):
        remote(phase, angles.at[k], ang_send.at[d], ang_recv.at[k], at_k(d)).start()
    angles[k] = phase[...]

    def norm_cols(j):
        lanes = pl.ds(j * 512, 512)

        def total(i, acc):
            x = cols[pl.ds(pl.multiple_of(i * 80, 16), 80), lanes].astype(F32)
            return acc + jnp.sum(x.reshape(10, 8, 512), axis=0)

        mean = jnp.sum(lax.fori_loop(0, 15, total, jnp.zeros((8, 512), F32)), axis=0, keepdims=True) * (1.0 / FRAMES)

        def squares(i, acc):
            x = cols[pl.ds(pl.multiple_of(i * 80, 16), 80), lanes].astype(F32) - mean
            return acc + jnp.sum((x * x).reshape(10, 8, 512), axis=0)

        scale = lax.rsqrt(jnp.sum(lax.fori_loop(0, 15, squares, jnp.zeros((8, 512), F32)), axis=0, keepdims=True) + EPS)

        def write(i, _):
            rows = pl.ds(pl.multiple_of(i * 80, 16), 80)
            cols[rows, lanes] = ((cols[rows, lanes].astype(F32) - mean) * scale).astype(BF16)
            return 0

        lax.fori_loop(0, 15, write, 0)

    def transform_cols(j):
        lanes = pl.ds(j * 256, 256)

        def block(i, _):
            rows = pl.ds(pl.multiple_of(i * 256, 256), 256)
            c = cols[:, lanes]
            kc[rows, lanes] = (dot(thi[rows, :], c) + dot(tlo[rows, :], c)).astype(BF16)
            return 0

        lax.fori_loop(0, 5, block, 0)

    series_copy.wait()
    norm_cols(0)

    a_me = lax.div(z + 16 - residue, 4)
    a_me = lax.rem(a_me, 4)

    def unit(da):
        return xx * 4 + lax.rem(a_me + da + 4, 4)

    @pl.when(hub)
    def _():
        chunks[k] = slab[pl.ds(pl.multiple_of(half * 16, 16), 16), :]
        for d in range(1, 8):
            src = lax.rem(k + d, 8)
            remote(chunks.at[src], chunks.at[src], chunk_send.at[0], chunk_recv.at[src], at_k(1)).wait_recv()
        x = jnp.concatenate([chunks[i] for i in range(8)], axis=1)
        x = x - jnp.sum(x, axis=1, keepdims=True) * (1.0 / FRAMES)
        u = unit(0)
        held[u] = jnp.concatenate([x, jnp.zeros((16, TP - FRAMES), F32)], axis=1).astype(BF16)
        for n, d in enumerate(NEAR):
            remote(held.at[u], held.at[u], near_send.at[n], unit_recv.at[u], at_z(d)).start()

    for order, da in enumerate((0, 1, -1, 2)):
        u = unit(da)
        got = remote(held.at[u], held.at[u], near_send.at[0], unit_recv.at[u], at_z(1))
        if da == 0:

            @pl.when(jnp.logical_not(hub))
            def _():
                got.wait_recv()

        else:
            got.wait_recv()
        if da == 1:

            @pl.when(hub)
            def _():
                for n, d in enumerate((-3, -2, -1)):
                    remote(held.at[u], held.at[u], relay_send.at[n], unit_recv.at[u], at_z(d)).start()

        if da == -1:

            @pl.when(hub)
            def _():
                for n, d in enumerate((4, 3, 2, 1)):
                    remote(held.at[u], held.at[u], relay_send.at[3 + n], unit_recv.at[u], at_z(d)).start()

        for n, d in enumerate((2, 1, 3)):
            remote(held.at[u], held.at[u], x_send.at[order * 3 + n], unit_recv.at[u], at_x(d)).start()
        if order == 0:
            norm_cols(1)
        elif order == 1:
            norm_cols(2)
            transform_cols(0)
        elif order == 2:
            transform_cols(1)
    for j in range(2, 6):
        transform_cols(j)

    for d in range(1, 8):
        src = lax.rem(k + d, 8)
        remote(angles.at[src], angles.at[src], ang_send.at[0], ang_recv.at[src], at_k(1)).wait_recv()
    turn = jnp.concatenate([angles[i] for i in range(8)] + [jnp.zeros((SURR, FP - FREQS), jnp.int32)], axis=1)
    angle = turn.astype(F32) * (2.0 * math.pi / FRAMES)
    lane = lax.broadcasted_iota(jnp.int32, (SURR, FP), 1)
    weight = jnp.where(lane < FREQS - 1, 1.0, jnp.where(lane == FREQS - 1, 0.5, 0.0)).astype(F32)
    cos_phase = jnp.cos(angle) * weight
    sin_phase = jnp.sin(angle) * weight

    for dx in range(1, 4):
        for a in range(4):
            u = lax.rem(xx + dx, 4) * 4 + a
            remote(held.at[u], held.at[u], near_send.at[0], unit_recv.at[u], at_x(dx)).wait_recv()

    xs = held[...].reshape(256, TP)
    for j in range(5):
        rows = pl.ds(j * 256, 256)
        spec[:, rows] = dot_t(xs, thi[rows, :]) + dot_t(xs, tlo[rows, :])
    lane1 = lax.broadcasted_iota(jnp.int32, (1, FP), 1)
    inner = (lane1 < FREQS - 1).astype(F32)
    sc = spec[:, 0:FP]
    ss = spec[:, FP:TP]
    power = jnp.sum((sc * sc + ss * ss) * inner, axis=1, keepdims=True)
    last = jnp.sum(jnp.where(lane1 == FREQS - 1, sc, 0.0), axis=1, keepdims=True)
    for s in range(SURR):
        cp = cos_phase[s : s + 1, :]
        sp = sin_phase[s : s + 1, :]
        rot[pl.ds(s * 256, 256), 0:FP] = (sc * cp + ss * sp).astype(BF16)
        rot[pl.ds(s * 256, 256), FP:TP] = (ss * cp - sc * sp).astype(BF16)

    best[...] = jnp.zeros_like(best)

    def correlate(j, _):
        lanes = pl.ds(pl.multiple_of(j * 256, 256), 256)
        right = kc[:, lanes]
        for s in range(SURR):
            rows = pl.ds(s * 256, 256)
            score = jnp.abs(dot(rot[rows, :], right))
            best[rows, :] = jnp.maximum(best[rows, :], jnp.maximum(score[:, :128], score[:, 128:]))
        return 0

    lax.fori_loop(0, 6, correlate, 0)

    lane128 = lax.broadcasted_iota(jnp.int32, (256, 128), 1)
    row16 = lax.rem(lax.broadcasted_iota(jnp.int32, (256, 128), 0), 16)
    placed = jnp.zeros((256, 128), F32)
    for s in range(SURR):
        end = 2.0 * cos_phase[s : s + 1, FREQS - 1 : FREQS] * last
        energy = power * (2.0 / FRAMES) + end * end * (1.0 / FRAMES)
        top = jnp.max(best[pl.ds(s * 256, 256), :], axis=1, keepdims=True)
        top = top * lax.rsqrt(energy + EPS) * (math.sqrt(FRAMES) * 2.0 / FRAMES)
        placed = jnp.where(lane128 == row16 + 16 * s, top, placed)
    mine[...] = jnp.max(placed.reshape(16, 16, 128), axis=1)

    for d in range(1, 8):
        remote(mine, parts.at[k], part_send.at[d], part_recv.at[k], at_k(d)).start()
    parts[k] = mine[...]
    for d in range(1, 8):
        src = lax.rem(k + d, 8)
        remote(parts.at[src], parts.at[src], part_send.at[0], part_recv.at[src], at_k(1)).wait_recv()
    lane16 = lax.broadcasted_iota(jnp.int32, (16, 128), 1)
    row_lane = lax.broadcasted_iota(jnp.int32, (1, 128), 1)
    top_row = jnp.zeros((1, 128), F32)
    for s in range(SURR):
        full = jnp.zeros((16, 128), F32)
        for kk in range(8):
            place = (kk % 4) * 32 + (kk // 4) * 16
            moved = pltpu.roll(parts[kk], (place - 16 * s) % 128, 1)
            full = jnp.where((lane16 >= place) & (lane16 < place + 16), moved, full)
        out_tile[pl.ds(s * 16, 16), :] = full
        top_row = jnp.where(row_lane == s, jnp.max(jnp.max(full, axis=0, keepdims=True), axis=1, keepdims=True), top_row)

    own_top[...] = top_row
    for n, d in enumerate(NEAR):
        remote(own_top, top1.at[n], t1_send.at[n], t1_recv.at[n], at_z(d)).start()
    for n, d in enumerate(NEAR):
        remote(own_top, top1.at[n], t1_send.at[n], t1_recv.at[n], at_z(d)).wait_recv()
    value = jnp.maximum(top_row, jnp.max(top1[...], axis=0))
    wide_top[...] = value
    for n, d in enumerate((4, -4)):
        remote(wide_top, top2.at[n], t2_send.at[n], t2_recv.at[n], at_z(d)).start()
    for n, d in enumerate((4, -4)):
        remote(wide_top, top2.at[n], t2_send.at[n], t2_recv.at[n], at_z(d)).wait_recv()
    value = jnp.maximum(value, jnp.max(top2[...], axis=0))
    line_top[...] = value
    for d in range(1, 4):
        remote(line_top, top3.at[d - 1], t3_send.at[d - 1], t3_recv.at[d - 1], at_x(d)).start()
    for d in range(1, 4):
        remote(line_top, top3.at[d - 1], t3_send.at[d - 1], t3_recv.at[d - 1], at_x(d)).wait_recv()
    out_peak[...] = jnp.maximum(value, jnp.max(top3[...], axis=0))

    for h in range(2):
        target = h * 4 + z_low

        @pl.when(target != k)
        def _():
            remote(slab.at[pl.ds(h * 16, 16)], chunks.at[k], chunk_send.at[h], chunk_recv.at[k], (col, target)).wait_send()

    for d in range(1, 8):
        remote(phase, angles.at[k], ang_send.at[d], ang_recv.at[k], at_k(d)).wait_send()
        remote(mine, parts.at[k], part_send.at[d], part_recv.at[k], at_k(d)).wait_send()

    @pl.when(hub)
    def _():
        u = unit(0)
        for n, d in enumerate(NEAR):
            remote(held.at[u], held.at[u], near_send.at[n], unit_recv.at[u], at_z(d)).wait_send()
        u = unit(1)
        for n, d in enumerate((-3, -2, -1)):
            remote(held.at[u], held.at[u], relay_send.at[n], unit_recv.at[u], at_z(d)).wait_send()
        u = unit(-1)
        for n, d in enumerate((4, 3, 2, 1)):
            remote(held.at[u], held.at[u], relay_send.at[3 + n], unit_recv.at[u], at_z(d)).wait_send()

    for order, da in enumerate((0, 1, -1, 2)):
        u = unit(da)
        for n, d in enumerate((2, 1, 3)):
            remote(held.at[u], held.at[u], x_send.at[order * 3 + n], unit_recv.at[u], at_x(d)).wait_send()
    for n, d in enumerate(NEAR):
        remote(own_top, top1.at[n], t1_send.at[n], t1_recv.at[n], at_z(d)).wait_send()
    for n, d in enumerate((4, -4)):
        remote(wide_top, top2.at[n], t2_send.at[n], t2_recv.at[n], at_z(d)).wait_send()
    for d in range(1, 4):
        remote(line_top, top3.at[d - 1], t3_send.at[d - 1], t3_recv.at[d - 1], at_x(d)).wait_send()


def body(series, slab_series, phase_index, basis):
    dma = pltpu.SemaphoreType.DMA
    vmem = pl.BlockSpec(memory_space=pltpu.VMEM)
    hbm = pl.BlockSpec(memory_space=pl.ANY)
    tile, peak = pl.pallas_call(
        kernel,
        out_shape=(jax.ShapeDtypeStruct((64, 128), F32), jax.ShapeDtypeStruct((1, 128), F32)),
        in_specs=[hbm, vmem, vmem, hbm],
        out_specs=(vmem, vmem),
        scratch_shapes=[
            pltpu.VMEM((TP, COLS), BF16),
            pltpu.VMEM((4, FP, 128), F32),
            pltpu.VMEM((TP, TP), BF16),
            pltpu.VMEM((TP, TP), BF16),
            pltpu.VMEM((TP, COLS), BF16),
            pltpu.VMEM((16, 16, TP), BF16),
            pltpu.VMEM((8, 16, 150), F32),
            pltpu.VMEM((8, SURR, 75), jnp.int32),
            pltpu.VMEM((256, TP), F32),
            pltpu.VMEM((1024, TP), BF16),
            pltpu.VMEM((1024, 128), F32),
            pltpu.VMEM((16, 128), F32),
            pltpu.VMEM((8, 16, 128), F32),
            pltpu.VMEM((1, 128), F32),
            pltpu.VMEM((8, 1, 128), F32),
            pltpu.VMEM((1, 128), F32),
            pltpu.VMEM((2, 1, 128), F32),
            pltpu.VMEM((1, 128), F32),
            pltpu.VMEM((3, 1, 128), F32),
            dma, dma, dma((2,)), dma((8,)), dma((8,)), dma((8,)), dma((8,)), dma((7,)), dma((12,)), dma((16,)),
            dma((8,)), dma((8,)), dma((8,)), dma((8,)), dma((2,)), dma((2,)), dma((3,)), dma((3,)),
        ],
        compiler_params=pltpu.CompilerParams(
            collective_id=0, has_side_effects=True, vmem_limit_bytes=56 * 1024 * 1024
        ),
        name="surrogate_peaks",
    )(series, slab_series.T, phase_index, basis)
    return tile.reshape(SURR, 2048)[:, :, None], peak[0, :SURR]


def solution(mesh):
    basis = basis_tables()

    def run(series, slab_series, phase_index):
        placed = (P(None, "col"), P("tm", "col"), P(None, "tm"), P())
        step = jax.shard_map(
            body, mesh=mesh, in_specs=placed, out_specs=(P(None, None, "col"), P()), check_vma=False
        )
        return step(series, slab_series, phase_index, jnp.asarray(basis))

    return run
```

time: 243 us -> 74.6 us (0.31)
  the two profiles are of different devices: /device:TPU:8 before, /device:TPU:1 now
where the time goes in v1:
time: 74.6 us; the launch traced here: 73.5 us
  Pallas kernels  70.4 us (94%)
  local copies, waits for them, and re-layouts  2.55 us (3%)
    pallas_call x1, Pallas kernels, body(): pl.pallas_call(kernel, out_shape=(jax.ShapeDtypeStruct((64, 128), F32), j...  70.4 us

profile of v1, /device:TPU:1, one launch (start us, length us, event | category | flops | bytes accessed | tf_op | source)
XLA Modules:
  0.0 73.5 jit_solution(5496093984297203715)
XLA Ops:
  0.6 70.4 %surrogate_peaks.1 = (f32[64,128]{1,0:T(8,128)}, f32[1,128]{1,0:T(1,128)}) custom-call(bf16[1200,1536]{1,0:T(8,128)(2,1)} %series.1, f32[32,150]{1,0:T(8,128)} %bitcast.4, s32[4,75]{1,0:T(4,128)} %phase.1, f32[4,640,128]{2,1,0:T(8,128)} %constant.2.clone.basis), custom_call_target="tpu_custom_call" | custom-call | tf_op jit(solution)/shard_map/surrogate_peaks/pallas_call | solution.py:336
  71.0 1.2 %slice_bitcast_fusion = f32[4]{0:T(128)} fusion(f32[1,128]{1,0:T(1,128)} %get-tuple-element.5), kind=kLoop, calls=%fused_computation | loop fusion | bytes 32 | tf_op jit(solution)/shard_map/squeeze | solution.py:369
  72.2 1.4 %copy.8 = f32[4,2048,1]{1,2,0:T(1,128)} copy(f32[4,2048,1]{1,2,0:T(1,128)} %bitcast.5) | data formatting | bytes 65536

commit v2 on v1

v2 whole, which is shorter than its diff:
```python
import functools
import math

import jax
import jax.numpy as jnp
import numpy as np
from jax import lax
from jax.experimental import pallas as pl
from jax.experimental.pallas import tpu as pltpu
from jax.sharding import PartitionSpec as P

FRAMES = 1200
FREQS = 600
FP = 640
TP = 1280
SURR = 4
COLS = 1536
EPS = 1e-6
F32 = jnp.float32
BF16 = jnp.bfloat16
MESH = pl.DeviceIdType.MESH
NEAR = (4, -4, 3, -3, 2, -2, 1, -1)


def basis_tables():
    freq = np.arange(1, FP + 1)[:, None]
    lane = np.arange(128)[None, :]
    fine = 2.0 * np.pi * ((freq * lane) % FRAMES) / FRAMES
    step = np.broadcast_to(2.0 * np.pi * ((freq * 128) % FRAMES) / FRAMES, fine.shape)
    return np.stack([np.cos(fine), np.sin(fine), np.cos(step), np.sin(step)]).astype(np.float32)


def dot(a, b):
    return lax.dot_general(a, b, (((1,), (0,)), ((), ())), preferred_element_type=F32)


def dot_t(a, b):
    return lax.dot_general(a, b, (((1,), (1,)), ((), ())), preferred_element_type=F32)


def kernel(
    series, slab, phase, basis, out_tile, out_peak,
    cols, bas, thi, tlo, kc, held, chunks, angles, spec, rot, best, mine, parts, own_top, top1, wide_top, top2, tile,
    own_sem, col_sem, bas_sem, chunk_send, chunk_recv, ang_send, ang_recv, near_send, relay_send, x_send, unit_recv,
    kc_send, kc_recv, part_send, part_recv, t1_send, t1_recv, t2_send, t2_recv, tile_sem,
):
    col = lax.axis_index("col")
    k = lax.axis_index("tm")
    xx = lax.div(col, 16)
    z = lax.rem(col, 16)
    residue = lax.rem(k, 4)
    half = lax.div(k, 4)
    core = lax.rem(k, 2)
    z_low = lax.rem(z, 4)
    hub = z_low == residue

    def at_z(d):
        return (xx * 16 + lax.rem(z + d + 16, 16), k)

    def at_x(d):
        return (lax.rem(xx + d, 4) * 16 + z, k)

    def at_xz(dx, dz):
        return (lax.rem(xx + dx, 4) * 16 + lax.rem(z + dz + 16, 16), k)

    def at_k(d):
        return (col, lax.rem(k + d, 8))

    def remote(src, dst, send, recv, dev):
        return pltpu.make_async_remote_copy(
            src_ref=src, dst_ref=dst, send_sem=send, recv_sem=recv, device_id=dev, device_id_type=MESH
        )

    def behind_of(d):
        return lax.div(lax.rem(z + d - residue + 32, 16), 4)

    behind = behind_of(0)

    def unit_to_z(rel, d):
        here = rel * 4 + xx
        there = lax.rem(behind + rel - behind_of(d) + 8, 4) * 4 + xx
        return here, there

    series_copy = pltpu.make_async_copy(
        series.at[:, pl.ds(pl.multiple_of(core * 768, 256), 768)], cols.at[pl.ds(0, FRAMES)], col_sem
    )
    basis_copy = pltpu.make_async_copy(basis, bas, bas_sem)
    own_phase = pltpu.make_async_copy(phase, angles.at[k], own_sem.at[0])
    own_chunk = pltpu.make_async_copy(slab.at[pl.ds(pl.multiple_of(half * 16, 16), 16)], chunks.at[k], own_sem.at[1])

    barrier = pltpu.get_barrier_semaphore()
    peers = [at_k(d) for d in range(1, 8)] + [at_x(d) for d in range(1, 4)] + [at_z(d) for d in NEAR]
    for dev in peers:
        pl.semaphore_signal(barrier, inc=1, device_id=dev, device_id_type=MESH)

    own_phase.start()
    own_chunk.start()
    basis_copy.start()
    series_copy.start()

    def make_rows(i, _):
        at = pl.multiple_of(i * 64, 64)
        c = bas[0, pl.ds(at, 64), :]
        s = bas[1, pl.ds(at, 64), :]
        sc = bas[2, pl.ds(at, 64), :]
        ss = bas[3, pl.ds(at, 64), :]
        for a in range(10):
            lanes = pl.ds(a * 128, 128)
            for base, val in ((0, c), (FP, s)):
                hi = val.astype(BF16)
                thi[pl.ds(base + at, 64), lanes] = hi
                tlo[pl.ds(base + at, 64), lanes] = (val - hi.astype(F32)).astype(BF16)
            c, s = c * sc - s * ss, s * sc + c * ss
        return 0

    def norm_cols():
        def total(i, acc):
            x = cols[pl.ds(pl.multiple_of(i * 80, 16), 80), :].astype(F32)
            return acc + jnp.sum(x.reshape(10, 8, 768), axis=0)

        mean = jnp.sum(lax.fori_loop(0, 15, total, jnp.zeros((8, 768), F32)), axis=0, keepdims=True) * (1.0 / FRAMES)

        def squares(i, acc):
            x = cols[pl.ds(pl.multiple_of(i * 80, 16), 80), :].astype(F32) - mean
            return acc + jnp.sum((x * x).reshape(10, 8, 768), axis=0)

        scale = lax.rsqrt(jnp.sum(lax.fori_loop(0, 15, squares, jnp.zeros((8, 768), F32)), axis=0, keepdims=True) + EPS)

        def write(i, _):
            rows = pl.ds(pl.multiple_of(i * 80, 16), 80)
            cols[rows, :] = ((cols[rows, :].astype(F32) - mean) * scale).astype(BF16)
            return 0

        lax.fori_loop(0, 15, write, 0)

    def kc_copy(i):
        block = kc.at[core * 3 + i]
        return remote(block, block, kc_send.at[i], kc_recv.at[core * 3 + i], (col, k + 1 - 2 * core))

    def transform_cols(i):
        lanes = pl.ds(i * 256, 256)

        def block(b, _):
            rows = pl.ds(pl.multiple_of(b * 640, 128), 640)
            c = cols[:, lanes]
            kc[core * 3 + i, rows, :] = (dot(thi[rows, :], c) + dot(tlo[rows, :], c)).astype(BF16)
            return 0

        lax.fori_loop(0, 2, block, 0)
        kc_copy(i).start()

    pl.semaphore_wait(barrier, 18)

    for h in range(2):
        target = h * 4 + z_low

        @pl.when(target != k)
        def _():
            remote(slab.at[pl.ds(h * 16, 16)], chunks.at[k], chunk_send.at[h], chunk_recv.at[k], (col, target)).start()

    for d in range(1, 8):
        remote(phase, angles.at[k], ang_send.at[d], ang_recv.at[k], at_k(d)).start()

    own_chunk.wait()
    own_phase.wait()
    basis_copy.wait()
    lax.fori_loop(0, 10, make_rows, 0)

    @pl.when(hub)
    def _():
        for d in range(1, 8):
            src = lax.rem(k + d, 8)
            remote(chunks.at[src], chunks.at[src], chunk_send.at[0], chunk_recv.at[src], at_k(1)).wait_recv()
        x = jnp.concatenate([chunks[i] for i in range(8)], axis=1)
        x = x - jnp.sum(x, axis=1, keepdims=True) * (1.0 / FRAMES)
        held[xx] = jnp.concatenate([x, jnp.zeros((16, TP - FRAMES), F32)], axis=1).astype(BF16)
        for n, d in enumerate(NEAR):
            here, there = unit_to_z(0, d)
            remote(held.at[here], held.at[there], near_send.at[n], unit_recv.at[there], at_z(d)).start()

    def arrived(rel):
        here = rel * 4 + xx
        remote(held.at[here], held.at[here], near_send.at[0], unit_recv.at[here], at_z(1)).wait_recv()

    def relay_copies(rel):
        copies = []
        for n, d in enumerate((-3, -2, -1) if rel == 1 else (4, 3, 2, 1)):
            here, there = unit_to_z(rel, d)
            send = relay_send.at[n if rel == 1 else 3 + n]
            copies.append(remote(held.at[here], held.at[there], send, unit_recv.at[there], at_z(d)))
        return copies

    def x_copies(rel):
        here = rel * 4 + xx
        return [
            remote(held.at[here], held.at[here], x_send.at[rel * 3 + n], unit_recv.at[here], at_x(d))
            for n, d in enumerate((2, 1, 3))
        ]

    def relay(rel):
        @pl.when(hub)
        def _():
            for copy in relay_copies(rel):
                copy.start()

    def forward(rel):
        for copy in x_copies(rel):
            copy.start()

    cols[pl.ds(FRAMES, TP - FRAMES), :] = jnp.zeros((TP - FRAMES, 768), BF16)
    series_copy.wait()

    @pl.when(hub)
    def _():
        forward(0)

    norm_cols()
    transform_cols(0)

    @pl.when(jnp.logical_not(hub))
    def _():
        arrived(0)
        forward(0)

    arrived(1)
    relay(1)
    forward(1)

    @pl.when(hub)
    def _():
        arrived(3)

    relay(3)
    transform_cols(1)

    @pl.when(jnp.logical_not(hub))
    def _():
        arrived(3)

    forward(3)
    transform_cols(2)
    arrived(2)
    forward(2)

    for d in range(1, 8):
        src = lax.rem(k + d, 8)
        remote(angles.at[src], angles.at[src], ang_send.at[0], ang_recv.at[src], at_k(1)).wait_recv()
    turn = jnp.concatenate([angles[i] for i in range(8)] + [jnp.zeros((SURR, FP - FREQS), jnp.int32)], axis=1)
    angle = turn.astype(F32) * (2.0 * math.pi / FRAMES)
    lane = lax.broadcasted_iota(jnp.int32, (SURR, FP), 1)
    weight = jnp.where(lane < FREQS - 1, 1.0, jnp.where(lane == FREQS - 1, 0.5, 0.0)).astype(F32)
    cos_phase = jnp.cos(angle) * weight
    sin_phase = jnp.sin(angle) * weight
    lane1 = lax.broadcasted_iota(jnp.int32, (1, FP), 1)
    inner = (lane1 < FREQS - 1).astype(F32)
    lane128 = lax.broadcasted_iota(jnp.int32, (128, 128), 1)
    row16 = lax.rem(lax.broadcasted_iota(jnp.int32, (128, 128), 0), 16)

    def vertices(h):
        for rel in (2 * h, 2 * h + 1):
            for dx in range(1, 4):
                slot = rel * 4 + lax.rem(xx + dx, 4)
                remote(held.at[slot], held.at[slot], near_send.at[0], unit_recv.at[slot], at_x(dx)).wait_recv()
        xs = held[8 * h : 8 * h + 8].reshape(128, TP)
        for j in range(5):
            rows = pl.ds(j * 256, 256)
            spec[:, rows] = dot_t(xs, thi[rows, :]) + dot_t(xs, tlo[rows, :])
        sc = spec[:, 0:FP]
        ss = spec[:, FP:TP]
        power = jnp.sum((sc * sc + ss * ss) * inner, axis=1, keepdims=True)
        last = jnp.sum(jnp.where(lane1 == FREQS - 1, sc, 0.0), axis=1, keepdims=True)
        for s in range(SURR):
            cp = cos_phase[s : s + 1, :]
            sp = sin_phase[s : s + 1, :]
            rot[pl.ds(s * 128, 128), 0:FP] = (sc * cp + ss * sp).astype(BF16)
            rot[pl.ds(s * 128, 128), FP:TP] = (ss * cp - sc * sp).astype(BF16)
        best[...] = jnp.zeros_like(best)
        if h == 0:
            for i in range(3):
                block = kc.at[(1 - core) * 3 + i]
                remote(block, block, kc_send.at[i], kc_recv.at[(1 - core) * 3 + i], at_k(1)).wait_recv()

        def correlate(j, _):
            score = jnp.abs(dot(rot[...], kc[j]))
            best[...] = jnp.maximum(best[...], jnp.maximum(score[:, :128], score[:, 128:]))
            return 0

        lax.fori_loop(0, 6, correlate, 0)
        placed = jnp.zeros((128, 128), F32)
        for s in range(SURR):
            end = 2.0 * cos_phase[s : s + 1, FREQS - 1 : FREQS] * last
            energy = power * (2.0 / FRAMES) + end * end * (1.0 / FRAMES)
            top = jnp.max(best[pl.ds(s * 128, 128), :], axis=1, keepdims=True)
            top = top * lax.rsqrt(energy + EPS) * (math.sqrt(FRAMES) * 2.0 / FRAMES)
            placed = jnp.where(lane128 == row16 + 16 * s, top, placed)
        found = jnp.max(placed.reshape(8, 16, 128), axis=1)
        for n in range(8):
            row = (n % 4) * 4 + lax.rem(behind + 2 * h + n // 4, 4)
            mine[pl.ds(row, 1), :] = found[n : n + 1, :]

    vertices(0)
    vertices(1)

    for d in range(1, 8):
        remote(mine, parts.at[k], part_send.at[d], part_recv.at[k], at_k(d)).start()
    parts[k] = mine[...]
    for d in range(1, 8):
        src = lax.rem(k + d, 8)
        remote(parts.at[src], parts.at[src], part_send.at[0], part_recv.at[src], at_k(1)).wait_recv()

    own_top[...] = jnp.max(jnp.max(parts[...], axis=0), axis=0, keepdims=True)
    for n, d in enumerate(NEAR):
        remote(own_top, top1.at[n], t1_send.at[n], t1_recv.at[n], at_z(d)).start()
    lane16 = lax.broadcasted_iota(jnp.int32, (16, 128), 1)
    for s in range(SURR):
        full = jnp.zeros((16, 128), F32)
        for kk in range(8):
            place = (kk % 4) * 32 + (kk // 4) * 16
            moved = pltpu.roll(parts[kk], (place - 16 * s) % 128, 1)
            full = jnp.where((lane16 >= place) & (lane16 < place + 16), moved, full)
        tile[pl.ds(s * 16, 16), :] = full
    tile_copy = pltpu.make_async_copy(tile, out_tile, tile_sem)
    tile_copy.start()
    for n, d in enumerate(NEAR):
        remote(own_top, top1.at[n], t1_send.at[n], t1_recv.at[n], at_z(d)).wait_recv()
    wide_top[...] = jnp.maximum(own_top[...], jnp.max(top1[...], axis=0))
    across = [(dx, dz) for dz in (4, -4) for dx in (2, 1, 3, 0)]
    for n, (dx, dz) in enumerate(across):
        remote(wide_top, top2.at[n], t2_send.at[n], t2_recv.at[n], at_xz(dx, dz)).start()
    for n, (dx, dz) in enumerate(across):
        remote(wide_top, top2.at[n], t2_send.at[n], t2_recv.at[n], at_xz(dx, dz)).wait_recv()
    every = jnp.max(top2[...], axis=0)
    row_lane = lax.broadcasted_iota(jnp.int32, (1, 128), 1)
    result = jnp.zeros((1, 128), F32)
    for s in range(SURR):
        inside = (row_lane >= 16 * s) & (row_lane < 16 * s + 16)
        result = jnp.where(row_lane == s, jnp.max(jnp.where(inside, every, 0.0), axis=1, keepdims=True), result)
    out_peak[...] = result

    tile_copy.wait()
    for h in range(2):
        target = h * 4 + z_low

        @pl.when(target != k)
        def _():
            remote(slab.at[pl.ds(h * 16, 16)], chunks.at[k], chunk_send.at[h], chunk_recv.at[k], (col, target)).wait_send()

    for d in range(1, 8):
        remote(phase, angles.at[k], ang_send.at[d], ang_recv.at[k], at_k(d)).wait_send()
        remote(mine, parts.at[k], part_send.at[d], part_recv.at[k], at_k(d)).wait_send()

    @pl.when(hub)
    def _():
        for n, d in enumerate(NEAR):
            here, there = unit_to_z(0, d)
            remote(held.at[here], held.at[there], near_send.at[n], unit_recv.at[there], at_z(d)).wait_send()
        for copy in relay_copies(1) + relay_copies(3):
            copy.wait_send()

    for rel in range(4):
        for copy in x_copies(rel):
            copy.wait_send()
    for i in range(3):
        kc_copy(i).wait_send()
    for n, d in enumerate(NEAR):
        remote(own_top, top1.at[n], t1_send.at[n], t1_recv.at[n], at_z(d)).wait_send()
    for n, (dx, dz) in enumerate(across):
        remote(wide_top, top2.at[n], t2_send.at[n], t2_recv.at[n], at_xz(dx, dz)).wait_send()


def body(series, slab_series, phase_index, basis):
    dma = pltpu.SemaphoreType.DMA
    vmem = pl.BlockSpec(memory_space=pltpu.VMEM)
    hbm = pl.BlockSpec(memory_space=pl.ANY)
    tile, peak = pl.pallas_call(
        kernel,
        out_shape=(jax.ShapeDtypeStruct((64, 128), F32), jax.ShapeDtypeStruct((1, 128), F32)),
        in_specs=[hbm, hbm, hbm, hbm],
        out_specs=(hbm, vmem),
        scratch_shapes=[
            pltpu.VMEM((TP, 768), BF16),
            pltpu.VMEM((4, FP, 128), F32),
            pltpu.VMEM((TP, TP), BF16),
            pltpu.VMEM((TP, TP), BF16),
            pltpu.VMEM((6, TP, 256), BF16),
            pltpu.VMEM((16, 16, TP), BF16),
            pltpu.VMEM((8, 16, 150), F32),
            pltpu.VMEM((8, SURR, 75), jnp.int32),
            pltpu.VMEM((128, TP), F32),
            pltpu.VMEM((512, TP), BF16),
            pltpu.VMEM((512, 128), F32),
            pltpu.VMEM((16, 128), F32),
            pltpu.VMEM((8, 16, 128), F32),
            pltpu.VMEM((1, 128), F32),
            pltpu.VMEM((8, 1, 128), F32),
            pltpu.VMEM((1, 128), F32),
            pltpu.VMEM((8, 1, 128), F32),
            pltpu.VMEM((64, 128), F32),
            dma((2,)), dma, dma, dma((2,)), dma((8,)), dma((8,)), dma((8,)), dma((8,)), dma((7,)), dma((12,)), dma((16,)),
            dma((3,)), dma((6,)), dma((8,)), dma((8,)), dma((8,)), dma((8,)), dma((8,)), dma((8,)), dma,
        ],
        compiler_params=pltpu.CompilerParams(
            collective_id=0, has_side_effects=True, vmem_limit_bytes=56 * 1024 * 1024
        ),
        name="surrogate_peaks",
    )(series, slab_series.T, phase_index, basis)
    return tile.reshape(SURR, 2048)[:, :, None], peak[0, :SURR]


def solution(mesh):
    basis = basis_tables()

    def run(series, slab_series, phase_index):
        placed = (P(None, "col"), P("tm", "col"), P(None, "tm"), P())
        step = jax.shard_map(
            body, mesh=mesh, in_specs=placed, out_specs=(P(None, None, "col"), P()), check_vma=False
        )
        return step(series, slab_series, phase_index, jnp.asarray(basis))

    return run
```

time: 74.6 us -> 61.1 us (0.82); the launches traced: 73.5 us -> 60.9 us
  Pallas kernels: 70.4 us -> 57.8 us
    pallas_call x1, Pallas kernels: 70.4 us -> 57.8 us  [body(): pl.pallas_call(kernel, out_shape=(jax.ShapeDtypeStruct((64, 128), F32), j...]
where the time goes in v2:
time: 61.1 us; the launch traced here: 60.9 us
  Pallas kernels  57.8 us (95%)
  local copies, waits for them, and re-layouts  2.55 us (4%)
  between operations  0.64 us (1%)
    pallas_call x1, Pallas kernels, body(): pl.pallas_call(kernel, out_shape=(jax.ShapeDtypeStruct((64, 128), F32), j...  57.8 us
    unnamed x1, local copies, waits for them, and re-layouts  1.37 us

profile of v2, /device:TPU:1, one launch (start us, length us, event | category | flops | bytes accessed | tf_op | source)
XLA Modules:
  0.0 60.9 jit_solution(3202064069090582943)
XLA Ops:
  0.6 57.8 %surrogate_peaks.1 = (f32[64,128]{1,0:T(8,128)}, f32[1,128]{1,0:T(1,128)}) custom-call(bf16[1200,1536]{1,0:T(8,128)(2,1)} %series.1, f32[32,150]{1,0:T(8,128)} %bitcast.4, s32[4,75]{1,0:T(4,128)} %phase.1, f32[4,640,128]{2,1,0:T(8,128)} %constant.2.clone.basis), custom_call_target="tpu_custom_call" | custom-call | tf_op jit(solution)/shard_map/surrogate_peaks/pallas_call | solution.py:375
  58.4 1.2 %slice_bitcast_fusion = f32[4]{0:T(128)} fusion(f32[1,128]{1,0:T(1,128)} %get-tuple-element.5), kind=kLoop, calls=%fused_computation | loop fusion | bytes 32 | tf_op jit(solution)/shard_map/squeeze | solution.py:407
  59.6 1.4 %copy.8 = f32[4,2048,1]{1,2,0:T(1,128)} copy(f32[4,2048,1]{1,2,0:T(1,128)} %bitcast.5) | data formatting | bytes 65536

commit v3 on v2

v3 whole, which is shorter than its diff:
```python
import functools
import math

import jax
import jax.numpy as jnp
import numpy as np
from jax import lax
from jax.experimental import pallas as pl
from jax.experimental.pallas import tpu as pltpu
from jax.sharding import PartitionSpec as P

FRAMES = 1200
FREQS = 600
FP = 640
TP = 1280
SURR = 4
COLS = 1536
EPS = 1e-6
F32 = jnp.float32
BF16 = jnp.bfloat16
MESH = pl.DeviceIdType.MESH
NEAR = (4, -4, 3, -3, 2, -2, 1, -1)
RING = (8, 7, -7, 6, -6, 5, -5, 4, -4, 3, -3, 2, -2, 1, -1)
PLANE = tuple((dx, dk) for dx in (2, 1, 3, 0) for dk in (4, 5, 3, 2, 6, 7, 1, 0) if (dx, dk) != (0, 0))


def basis_tables():
    freq = np.arange(1, FP + 1)[:, None]
    lane = np.arange(128)[None, :]
    fine = 2.0 * np.pi * ((freq * lane) % FRAMES) / FRAMES
    step = np.broadcast_to(2.0 * np.pi * ((freq * 128) % FRAMES) / FRAMES, fine.shape)
    return np.stack([np.cos(fine), np.sin(fine), np.cos(step), np.sin(step)]).astype(np.float32)


def dot(a, b):
    return lax.dot_general(a, b, (((1,), (0,)), ((), ())), preferred_element_type=F32)


def dot_t(a, b):
    return lax.dot_general(a, b, (((1,), (1,)), ((), ())), preferred_element_type=F32)


def kernel(
    series, slab, phase, basis, out_tile, out_peak,
    cols, bas, thi, tlo, kc, held, chunks, angles, spec, rot, best, mine, parts, own_top, top1, wide_top, top2,
    own_sem, col_sem, bas_sem, chunk_send, chunk_recv, ang_send, ang_recv, near_send, relay_send, x_send, unit_recv,
    kc_send, kc_recv, part_send, part_recv, t1_send, t1_recv, t2_send, t2_recv, hello,
):
    col = lax.axis_index("col")
    k = lax.axis_index("tm")
    xx = lax.div(col, 16)
    z = lax.rem(col, 16)
    residue = lax.rem(k, 4)
    half = lax.div(k, 4)
    core = lax.rem(k, 2)
    z_low = lax.rem(z, 4)
    hub = z_low == residue

    def at_z(d):
        return (xx * 16 + lax.rem(z + d + 16, 16), k)

    def at_x(d):
        return (lax.rem(xx + d, 4) * 16 + z, k)

    def at_xk(dx, dk):
        return (lax.rem(xx + dx, 4) * 16 + z, lax.rem(k + dk, 8))

    def at_k(d):
        return (col, lax.rem(k + d, 8))

    def remote(src, dst, send, recv, dev):
        return pltpu.make_async_remote_copy(
            src_ref=src, dst_ref=dst, send_sem=send, recv_sem=recv, device_id=dev, device_id_type=MESH
        )

    def await_sent(ref, sem):
        remote(ref, ref, sem, sem, at_k(1)).wait_send()

    def await_all(ref, sem):
        remote(ref, ref, sem, sem, at_k(1)).wait_recv()

    def behind_of(d):
        return lax.div(lax.rem(z + d - residue + 32, 16), 4)

    behind = behind_of(0)

    def unit_to_z(rel, d):
        here = rel * 4 + xx
        there = lax.rem(behind + rel - behind_of(d) + 8, 4) * 4 + xx
        return here, there

    series_copy = pltpu.make_async_copy(
        series.at[:, pl.ds(pl.multiple_of(core * 768, 256), 768)], cols.at[pl.ds(0, FRAMES)], col_sem
    )
    basis_copy = pltpu.make_async_copy(basis, bas, bas_sem)
    own_phase = pltpu.make_async_copy(phase, angles.at[k], own_sem.at[0])
    own_chunk = pltpu.make_async_copy(slab.at[pl.ds(pl.multiple_of(half * 16, 16), 16)], chunks.at[k], own_sem.at[1])

    barrier = pltpu.get_barrier_semaphore()
    peers = [at_k(d) for d in range(1, 8)] + [at_x(d) for d in range(1, 4)] + [at_z(d) for d in (2, -2, 1, -1)]
    for dev in peers:
        pl.semaphore_signal(barrier, inc=1, device_id=dev, device_id_type=MESH)

    own_phase.start()
    own_chunk.start()
    basis_copy.start()
    series_copy.start()

    def make_rows(i, _):
        at = pl.multiple_of(i * 64, 64)
        c = bas[0, pl.ds(at, 64), :]
        s = bas[1, pl.ds(at, 64), :]
        sc = bas[2, pl.ds(at, 64), :]
        ss = bas[3, pl.ds(at, 64), :]
        for a in range(10):
            lanes = pl.ds(a * 128, 128)
            for base, val in ((0, c), (FP, s)):
                hi = val.astype(BF16)
                thi[pl.ds(base + at, 64), lanes] = hi
                tlo[pl.ds(base + at, 64), lanes] = (val - hi.astype(F32)).astype(BF16)
            c, s = c * sc - s * ss, s * sc + c * ss
        return 0

    def norm_cols():
        def total(i, acc):
            x = cols[pl.ds(pl.multiple_of(i * 80, 16), 80), :].astype(F32)
            return acc + jnp.sum(x.reshape(10, 8, 768), axis=0)

        mean = jnp.sum(lax.fori_loop(0, 15, total, jnp.zeros((8, 768), F32)), axis=0, keepdims=True) * (1.0 / FRAMES)

        def squares(i, acc):
            x = cols[pl.ds(pl.multiple_of(i * 80, 16), 80), :].astype(F32) - mean
            return acc + jnp.sum((x * x).reshape(10, 8, 768), axis=0)

        scale = lax.rsqrt(jnp.sum(lax.fori_loop(0, 15, squares, jnp.zeros((8, 768), F32)), axis=0, keepdims=True) + EPS)

        def write(i, _):
            rows = pl.ds(pl.multiple_of(i * 80, 16), 80)
            cols[rows, :] = ((cols[rows, :].astype(F32) - mean) * scale).astype(BF16)
            return 0

        lax.fori_loop(0, 15, write, 0)

    def kc_copy(i):
        block = kc.at[core * 3 + i]
        return remote(block, block, kc_send, kc_recv, (col, k + 1 - 2 * core))

    def transform_cols(i):
        lanes = pl.ds(i * 256, 256)

        def block(b, _):
            rows = pl.ds(pl.multiple_of(b * 640, 128), 640)
            c = cols[:, lanes]
            kc[core * 3 + i, rows, :] = (dot(thi[rows, :], c) + dot(tlo[rows, :], c)).astype(BF16)
            return 0

        lax.fori_loop(0, 2, block, 0)
        kc_copy(i).start()

    pl.semaphore_wait(barrier, 14)

    for h in range(2):
        target = h * 4 + z_low

        @pl.when(target != k)
        def _():
            remote(slab.at[pl.ds(h * 16, 16)], chunks.at[k], chunk_send.at[h], chunk_recv, (col, target)).start()

    for d in (2, -2):
        pl.semaphore_signal(hello, inc=1, device_id=at_z(d), device_id_type=MESH)
    for d in range(1, 8):
        remote(phase, angles.at[k], ang_send, ang_recv, at_k(d)).start()

    basis_copy.wait()
    lax.fori_loop(0, 10, make_rows, 0)
    own_chunk.wait()
    own_phase.wait()
    pl.semaphore_wait(hello, 2)

    @pl.when(hub)
    def _():
        await_all(chunks.at[pl.ds(0, 7)], chunk_recv)
        x = jnp.concatenate([chunks[i] for i in range(8)], axis=1)
        x = x - jnp.sum(x, axis=1, keepdims=True) * (1.0 / FRAMES)
        held[xx] = jnp.concatenate([x, jnp.zeros((16, TP - FRAMES), F32)], axis=1).astype(BF16)
        for n, d in enumerate(NEAR):
            here, there = unit_to_z(0, d)
            remote(held.at[here], held.at[there], near_send, unit_recv.at[there], at_z(d)).start()

    def arrived(rel):
        here = rel * 4 + xx
        remote(held.at[here], held.at[here], near_send, unit_recv.at[here], at_z(1)).wait_recv()

    def relay_copies(rel):
        copies = []
        for d in (-3, -2, -1) if rel == 1 else (4, 3, 2, 1):
            here, there = unit_to_z(rel, d)
            copies.append(remote(held.at[here], held.at[there], relay_send, unit_recv.at[there], at_z(d)))
        return copies

    def x_copies(rel):
        here = rel * 4 + xx
        return [
            remote(held.at[here], held.at[here], x_send, unit_recv.at[here], at_x(d))
            for d in (2, 1, 3)
        ]

    def relay(rel):
        for copy in relay_copies(rel):
            copy.start()

    def forward(rel):
        for copy in x_copies(rel):
            copy.start()

    @pl.when(hub)
    def _():
        forward(0)

    cols[pl.ds(FRAMES, TP - FRAMES), :] = jnp.zeros((TP - FRAMES, 768), BF16)
    series_copy.wait()
    norm_cols()

    turned = lax.rem(lax.div(behind + 1, 2), 2)

    def neighbour(rel):
        arrived(rel)
        relay(rel)
        forward(rel)

    transform_cols(0)

    @pl.when(jnp.logical_not(hub))
    def _():
        arrived(0)
        forward(0)

    @pl.when(hub & (turned == 0))
    def _():
        neighbour(1)

    @pl.when(hub & (turned == 1))
    def _():
        neighbour(3)

    transform_cols(1)

    @pl.when(hub & (turned == 0))
    def _():
        neighbour(3)

    @pl.when(hub & (turned == 1))
    def _():
        neighbour(1)

    @pl.when(jnp.logical_not(hub))
    def _():
        arrived(1)
        forward(1)

    transform_cols(2)

    @pl.when(jnp.logical_not(hub))
    def _():
        arrived(3)
        forward(3)

    arrived(2)
    forward(2)

    await_all(angles.at[pl.ds(0, 7)], ang_recv)
    turn = jnp.concatenate([angles[i] for i in range(8)] + [jnp.zeros((SURR, FP - FREQS), jnp.int32)], axis=1)
    angle = turn.astype(F32) * (2.0 * math.pi / FRAMES)
    lane = lax.broadcasted_iota(jnp.int32, (SURR, FP), 1)
    weight = jnp.where(lane < FREQS - 1, 1.0, jnp.where(lane == FREQS - 1, 0.5, 0.0)).astype(F32)
    cos_phase = jnp.cos(angle) * weight
    sin_phase = jnp.sin(angle) * weight
    lane1 = lax.broadcasted_iota(jnp.int32, (1, FP), 1)
    inner = (lane1 < FREQS - 1).astype(F32)
    lane128 = lax.broadcasted_iota(jnp.int32, (256, 128), 1)
    row16 = lax.rem(lax.broadcasted_iota(jnp.int32, (256, 128), 0), 16)

    def spectra(h):
        for rel in ((0, 1), (3, 2))[h]:
            for dx in range(1, 4):
                slot = rel * 4 + lax.rem(xx + dx, 4)
                await_all(held.at[slot], unit_recv.at[slot])
        xs = held[8 * h : 8 * h + 8].reshape(128, TP)
        for j in range(5):
            rows = pl.ds(j * 256, 256)
            spec[pl.ds(128 * h, 128), rows] = dot_t(xs, thi[rows, :]) + dot_t(xs, tlo[rows, :])

    def rotate(h, s):
        sc = spec[pl.ds(128 * h, 128), 0:FP]
        ss = spec[pl.ds(128 * h, 128), FP:TP]
        cp = cos_phase[s : s + 1, :]
        sp = sin_phase[s : s + 1, :]
        rows = pl.ds(s * 256 + 128 * h, 128)
        rot[rows, 0:FP] = (sc * cp + ss * sp).astype(BF16)
        rot[rows, FP:TP] = (ss * cp - sc * sp).astype(BF16)

    spectra(0)
    for s in range(SURR):
        rotate(0, s)
    await_all(kc.at[pl.ds(0, 3)], kc_recv)
    spectra(1)
    for s in range(SURR):
        rotate(1, s)
        rows = pl.ds(s * 256, 256)
        for j in range(6):
            score = jnp.abs(dot(rot[rows, :], kc[j]))
            score = jnp.maximum(score[:, :128], score[:, 128:])
            best[rows, :] = score if j == 0 else jnp.maximum(best[rows, :], score)
    sc = spec[:, 0:FP]
    ss = spec[:, FP:TP]
    power = jnp.sum((sc * sc + ss * ss) * inner, axis=1, keepdims=True)
    last = jnp.sum(jnp.where(lane1 == FREQS - 1, sc, 0.0), axis=1, keepdims=True)
    placed = jnp.zeros((256, 128), F32)
    for s in range(SURR):
        end = 2.0 * cos_phase[s : s + 1, FREQS - 1 : FREQS] * last
        energy = power * (2.0 / FRAMES) + end * end * (1.0 / FRAMES)
        top = jnp.max(best[pl.ds(s * 256, 256), :], axis=1, keepdims=True)
        top = top * lax.rsqrt(energy + EPS) * (math.sqrt(FRAMES) * 2.0 / FRAMES)
        placed = jnp.where(lane128 == row16 + 16 * s, top, placed)
    found = jnp.max(placed.reshape(16, 16, 128), axis=1)
    for n in range(16):
        row = (n % 4) * 4 + lax.rem(behind + n // 4, 4)
        mine[pl.ds(row, 1), :] = found[n : n + 1, :]

    own_top[...] = jnp.max(mine[...], axis=0, keepdims=True)
    for n, (dx, dk) in enumerate(PLANE):
        remote(own_top, top1.at[n], t1_send, t1_recv, at_xk(dx, dk)).start()
    for d in range(1, 8):
        remote(mine, parts.at[k], part_send, part_recv, at_k(d)).start()
    parts[k] = mine[...]
    await_all(top1, t1_recv)
    wide_top[...] = jnp.maximum(own_top[...], jnp.max(top1[...], axis=0))
    for n, d in enumerate(RING):
        remote(wide_top, top2.at[n], t2_send, t2_recv, at_z(d)).start()
    await_all(parts.at[pl.ds(0, 7)], part_recv)
    lane16 = lax.broadcasted_iota(jnp.int32, (16, 128), 1)
    for s in range(SURR):
        full = jnp.zeros((16, 128), F32)
        for kk in range(8):
            place = (kk % 4) * 32 + (kk // 4) * 16
            moved = pltpu.roll(parts[kk], (place - 16 * s) % 128, 1)
            full = jnp.where((lane16 >= place) & (lane16 < place + 16), moved, full)
        out_tile[pl.ds(s * 16, 16), :] = full
    await_all(top2, t2_recv)
    every = jnp.maximum(wide_top[...], jnp.max(top2[...], axis=0))
    row_lane = lax.broadcasted_iota(jnp.int32, (1, 128), 1)
    result = jnp.zeros((1, 128), F32)
    for s in range(SURR):
        inside = (row_lane >= 16 * s) & (row_lane < 16 * s + 16)
        result = jnp.where(row_lane == s, jnp.max(jnp.where(inside, every, 0.0), axis=1, keepdims=True), result)
    out_peak[...] = result

    for h in range(2):
        target = h * 4 + z_low

        @pl.when(target != k)
        def _():
            remote(slab.at[pl.ds(h * 16, 16)], chunks.at[k], chunk_send.at[h], chunk_recv, (col, target)).wait_send()

    @pl.when(hub)
    def _():
        await_sent(held.at[pl.ds(0, 8)], near_send)
        await_sent(held.at[pl.ds(0, 7)], relay_send)

    await_sent(angles.at[pl.ds(0, 7)], ang_send)
    await_sent(held.at[pl.ds(0, 12)], x_send)
    await_sent(kc.at[pl.ds(0, 3)], kc_send)
    await_sent(parts.at[pl.ds(0, 7)], part_send)
    await_sent(top1, t1_send)
    await_sent(top2, t2_send)


def body(series, slab_series, phase_index, basis):
    dma = pltpu.SemaphoreType.DMA
    vmem = pl.BlockSpec(memory_space=pltpu.VMEM)
    hbm = pl.BlockSpec(memory_space=pl.ANY)
    tile, peak = pl.pallas_call(
        kernel,
        out_shape=(pltpu.VMEM((64, 128), F32), pltpu.VMEM((1, 128), F32)),
        in_specs=[hbm, hbm, hbm, hbm],
        out_specs=(vmem, vmem),
        scratch_shapes=[
            pltpu.VMEM((TP, 768), BF16),
            pltpu.VMEM((4, FP, 128), F32),
            pltpu.VMEM((TP, TP), BF16),
            pltpu.VMEM((TP, TP), BF16),
            pltpu.VMEM((6, TP, 256), BF16),
            pltpu.VMEM((16, 16, TP), BF16),
            pltpu.VMEM((8, 16, 150), F32),
            pltpu.VMEM((8, SURR, 75), jnp.int32),
            pltpu.VMEM((256, TP), F32),
            pltpu.VMEM((1024, TP), BF16),
            pltpu.VMEM((1024, 128), F32),
            pltpu.VMEM((16, 128), F32),
            pltpu.VMEM((8, 16, 128), F32),
            pltpu.VMEM((1, 128), F32),
            pltpu.VMEM((31, 1, 128), F32),
            pltpu.VMEM((1, 128), F32),
            pltpu.VMEM((15, 1, 128), F32),
            dma((2,)), dma, dma, dma((2,)), dma, dma, dma, dma, dma, dma, dma((16,)),
            dma, dma, dma, dma, dma, dma, dma, dma, pltpu.SemaphoreType.REGULAR,
        ],
        compiler_params=pltpu.CompilerParams(
            collective_id=0, has_side_effects=True, vmem_limit_bytes=56 * 1024 * 1024
        ),
        name="surrogate_peaks",
    )(series, slab_series.T, phase_index, basis)
    return tile.reshape(SURR, 2048)[:, :, None], peak[0, :SURR]


def solution(mesh):
    basis = basis_tables()

    def run(series, slab_series, phase_index):
        placed = (P(None, "col"), P("tm", "col"), P(None, "tm"), P())
        step = jax.shard_map(
            body, mesh=mesh, in_specs=placed, out_specs=(P(None, None, "col"), P()), check_vma=False
        )
        return step(series, slab_series, phase_index, jnp.asarray(basis))

    return run
```

time: 61.1 us -> 53.1 us (0.87)
  Pallas kernels: 57.8 us -> 51.3 us
  local copies, waits for them, and re-layouts: 2.55 us -> 1.13 us
    pallas_call x1, Pallas kernels: 57.8 us -> 51.3 us  [body(): pl.pallas_call(kernel, out_shape=(pltpu.VMEM((64, 128), F32), pltpu.VMEM(...]
    unnamed x1, local copies, waits for them, and re-layouts: 1.37 us -> 0.62 us
    squeeze x1, local copies, waits for them, and re-layouts: 1.18 us -> 0.51 us  [body(): return (tile.reshape(SURR, 2048)[:, :, None], peak[0, :SURR])]
where the time goes in v3:
time: 53.1 us; the launch traced here: 53 us
  Pallas kernels  51.3 us (97%)
  local copies, waits for them, and re-layouts  1.13 us (2%)
  between operations  0.64 us (1%)
    pallas_call x1, Pallas kernels, body(): pl.pallas_call(kernel, out_shape=(pltpu.VMEM((64, 128), F32), pltpu.VMEM(...  51.3 us

profile of v3, /device:TPU:1, one launch (start us, length us, event | category | flops | bytes accessed | tf_op | source)
XLA Modules:
  0.0 53.0 jit_solution(523079524134312091)
XLA Ops:
  0.6 51.3 %surrogate_peaks.1 = (f32[64,128]{1,0:T(8,128)S(1)}, f32[1,128]{1,0:T(1,128)S(1)}) custom-call(bf16[1200,1536]{1,0:T(8,128)(2,1)} %series.1, f32[32,150]{1,0:T(8,128)} %bitcast.5, s32[4,75]{1,0:T(4,128)} %phase.1, f32[4,640,128]{2,1,0:T(8,128)} %constant.2.clone.basis), custom_call_target="tpu_custom_call" | custom-call | tf_op jit(solution)/shard_map/surrogate_peaks/pallas_call | solution.py:382
  51.9 0.6 %copy.8 = f32[4,2048,1]{1,2,0:T(1,128)} copy(f32[4,2048,1]{1,2,0:T(1,128)S(1)} %bitcast.4) | data formatting | bytes 65536
  52.5 0.5 slice_bitcast_fusion

commit v4 on v3

--- a/solution.py
+++ b/solution.py
@@ -42,15 +42,15 @@
 
 def kernel(
     series, slab, phase, basis, out_tile, out_peak,
-    cols, bas, thi, tlo, kc, held, chunks, angles, spec, rot, best, mine, parts, own_top, top1, wide_top, top2,
-    own_sem, col_sem, bas_sem, chunk_send, chunk_recv, ang_send, ang_recv, near_send, relay_send, x_send, unit_recv,
+    cols, bas, thi, tlo, kc, held, block_rows, chunks, angles, spec, rot, best, mine, parts, own_top, top1, wide_top, top2,
+    own_sem, col_sem, bas_sem, chunk_send, chunk_recv, ang_send, ang_recv, near_send, relay_send, x_send, x_recv, unit_recv,
     kc_send, kc_recv, part_send, part_recv, t1_send, t1_recv, t2_send, t2_recv, hello,
 ):
     col = lax.axis_index("col")
     k = lax.axis_index("tm")
     xx = lax.div(col, 16)
     z = lax.rem(col, 16)
-    residue = lax.rem(k, 4)
+    residue = lax.rem(k, 2) * 2 + lax.div(lax.rem(k, 4), 2)
     half = lax.div(k, 4)
     core = lax.rem(k, 2)
     z_low = lax.rem(z, 4)
@@ -94,7 +94,7 @@
     )
     basis_copy = pltpu.make_async_copy(basis, bas, bas_sem)
     own_phase = pltpu.make_async_copy(phase, angles.at[k], own_sem.at[0])
-    own_chunk = pltpu.make_async_copy(slab.at[pl.ds(pl.multiple_of(half * 16, 16), 16)], chunks.at[k], own_sem.at[1])
+    own_chunk = pltpu.make_async_copy(slab, block_rows, own_sem.at[1])
 
     barrier = pltpu.get_barrier_semaphore()
     peers = [at_k(d) for d in range(1, 8)] + [at_x(d) for d in range(1, 4)] + [at_z(d) for d in (2, -2, 1, -1)]
@@ -157,14 +157,15 @@
         lax.fori_loop(0, 2, block, 0)
         kc_copy(i).start()
 
+    own_chunk.wait()
     pl.semaphore_wait(barrier, 14)
 
     for h in range(2):
-        target = h * 4 + z_low
+        target = h * 4 + lax.rem(z_low, 2) * 2 + lax.div(z_low, 2)
 
         @pl.when(target != k)
         def _():
-            remote(slab.at[pl.ds(h * 16, 16)], chunks.at[k], chunk_send.at[h], chunk_recv, (col, target)).start()
+            remote(block_rows.at[pl.ds(h * 16, 16)], chunks.at[k], chunk_send.at[h], chunk_recv, (col, target)).start()
 
     for d in (2, -2):
         pl.semaphore_signal(hello, inc=1, device_id=at_z(d), device_id_type=MESH)
@@ -173,37 +174,37 @@
 
     basis_copy.wait()
     lax.fori_loop(0, 10, make_rows, 0)
-    own_chunk.wait()
     own_phase.wait()
     pl.semaphore_wait(hello, 2)
 
+    def send_own(hops):
+        for d in hops:
+            here, there = unit_to_z(0, d)
+            remote(held.at[here], held.at[there], near_send, unit_recv.at[lax.div(there, 4)], at_z(d)).start()
+
     @pl.when(hub)
     def _():
+        chunks[k] = block_rows[pl.ds(pl.multiple_of(half * 16, 16), 16), :]
         await_all(chunks.at[pl.ds(0, 7)], chunk_recv)
         x = jnp.concatenate([chunks[i] for i in range(8)], axis=1)
         x = x - jnp.sum(x, axis=1, keepdims=True) * (1.0 / FRAMES)
         held[xx] = jnp.concatenate([x, jnp.zeros((16, TP - FRAMES), F32)], axis=1).astype(BF16)
-        for n, d in enumerate(NEAR):
-            here, there = unit_to_z(0, d)
-            remote(held.at[here], held.at[there], near_send, unit_recv.at[there], at_z(d)).start()
+        send_own(NEAR)
 
     def arrived(rel):
         here = rel * 4 + xx
-        remote(held.at[here], held.at[here], near_send, unit_recv.at[here], at_z(1)).wait_recv()
+        remote(held.at[here], held.at[here], near_send, unit_recv.at[rel], at_z(1)).wait_recv()
 
     def relay_copies(rel):
         copies = []
         for d in (-3, -2, -1) if rel == 1 else (4, 3, 2, 1):
             here, there = unit_to_z(rel, d)
-            copies.append(remote(held.at[here], held.at[there], relay_send, unit_recv.at[there], at_z(d)))
+            copies.append(remote(held.at[here], held.at[there], relay_send, unit_recv.at[lax.div(there, 4)], at_z(d)))
         return copies
 
-    def x_copies(rel):
+    def x_copies(rel, hops=(2, 1, 3)):
         here = rel * 4 + xx
-        return [
-            remote(held.at[here], held.at[here], x_send, unit_recv.at[here], at_x(d))
-            for d in (2, 1, 3)
-        ]
+        return [remote(held.at[here], held.at[here], x_send, x_recv.at[rel // 2], at_x(d)) for d in hops]
 
     def relay(rel):
         for copy in relay_copies(rel):
@@ -238,20 +239,14 @@
     @pl.when(hub & (turned == 0))
     def _():
         neighbour(1)
+        neighbour(3)
 
     @pl.when(hub & (turned == 1))
     def _():
         neighbour(3)
+        neighbour(1)
 
     transform_cols(1)
-
-    @pl.when(hub & (turned == 0))
-    def _():
-        neighbour(3)
-
-    @pl.when(hub & (turned == 1))
-    def _():
-        neighbour(1)
 
     @pl.when(jnp.logical_not(hub))
     def _():
@@ -263,10 +258,17 @@
     @pl.when(jnp.logical_not(hub))
     def _():
         arrived(3)
-        forward(3)
-
-    arrived(2)
-    forward(2)
+        x_copies(3, (2,))[0].start()
+        arrived(2)
+        x_copies(2, (2,))[0].start()
+        for rel in (3, 2):
+            for copy in x_copies(rel, (1, 3)):
+                copy.start()
+
+    @pl.when(hub)
+    def _():
+        arrived(2)
+        forward(2)
 
     await_all(angles.at[pl.ds(0, 7)], ang_recv)
     turn = jnp.concatenate([angles[i] for i in range(8)] + [jnp.zeros((SURR, FP - FREQS), jnp.int32)], axis=1)
@@ -281,10 +283,7 @@
     row16 = lax.rem(lax.broadcasted_iota(jnp.int32, (256, 128), 0), 16)
 
     def spectra(h):
-        for rel in ((0, 1), (3, 2))[h]:
-            for dx in range(1, 4):
-                slot = rel * 4 + lax.rem(xx + dx, 4)
-                await_all(held.at[slot], unit_recv.at[slot])
+        await_all(held.at[pl.ds(0, 6)], x_recv.at[h])
         xs = held[8 * h : 8 * h + 8].reshape(128, TP)
         for j in range(5):
             rows = pl.ds(j * 256, 256)
@@ -304,6 +303,15 @@
         rotate(0, s)
     await_all(kc.at[pl.ds(0, 3)], kc_recv)
     spectra(1)
+    sc = spec[:, 0:FP]
+    ss = spec[:, FP:TP]
+    power = jnp.sum((sc * sc + ss * ss) * inner, axis=1, keepdims=True)
+    last = jnp.sum(jnp.where(lane1 == FREQS - 1, sc, 0.0), axis=1, keepdims=True)
+    scales = []
+    for s in range(SURR):
+        end = 2.0 * cos_phase[s : s + 1, FREQS - 1 : FREQS] * last
+        energy = power * (2.0 / FRAMES) + end * end * (1.0 / FRAMES)
+        scales.append(lax.rsqrt(energy + EPS) * (math.sqrt(FRAMES) * 2.0 / FRAMES))
     for s in range(SURR):
         rotate(1, s)
         rows = pl.ds(s * 256, 256)
@@ -311,16 +319,9 @@
             score = jnp.abs(dot(rot[rows, :], kc[j]))
             score = jnp.maximum(score[:, :128], score[:, 128:])
             best[rows, :] = score if j == 0 else jnp.maximum(best[rows, :], score)
-    sc = spec[:, 0:FP]
-    ss = spec[:, FP:TP]
-    power = jnp.sum((sc * sc + ss * ss) * inner, axis=1, keepdims=True)
-    last = jnp.sum(jnp.where(lane1 == FREQS - 1, sc, 0.0), axis=1, keepdims=True)
     placed = jnp.zeros((256, 128), F32)
     for s in range(SURR):
-        end = 2.0 * cos_phase[s : s + 1, FREQS - 1 : FREQS] * last
-        energy = power * (2.0 / FRAMES) + end * end * (1.0 / FRAMES)
-        top = jnp.max(best[pl.ds(s * 256, 256), :], axis=1, keepdims=True)
-        top = top * lax.rsqrt(energy + EPS) * (math.sqrt(FRAMES) * 2.0 / FRAMES)
+        top = jnp.max(best[pl.ds(s * 256, 256), :], axis=1, keepdims=True) * scales[s]
         placed = jnp.where(lane128 == row16 + 16 * s, top, placed)
     found = jnp.max(placed.reshape(16, 16, 128), axis=1)
     for n in range(16):
@@ -342,7 +343,7 @@
     for s in range(SURR):
         full = jnp.zeros((16, 128), F32)
         for kk in range(8):
-            place = (kk % 4) * 32 + (kk // 4) * 16
+            place = (kk % 2 * 2 + kk % 4 // 2) * 32 + (kk // 4) * 16
             moved = pltpu.roll(parts[kk], (place - 16 * s) % 128, 1)
             full = jnp.where((lane16 >= place) & (lane16 < place + 16), moved, full)
         out_tile[pl.ds(s * 16, 16), :] = full
@@ -356,11 +357,11 @@
     out_peak[...] = result
 
     for h in range(2):
-        target = h * 4 + z_low
+        target = h * 4 + lax.rem(z_low, 2) * 2 + lax.div(z_low, 2)
 
         @pl.when(target != k)
         def _():
-            remote(slab.at[pl.ds(h * 16, 16)], chunks.at[k], chunk_send.at[h], chunk_recv, (col, target)).wait_send()
+            remote(block_rows.at[pl.ds(h * 16, 16)], chunks.at[k], chunk_send.at[h], chunk_recv, (col, target)).wait_send()
 
     @pl.when(hub)
     def _():
@@ -391,6 +392,7 @@
             pltpu.VMEM((TP, TP), BF16),
             pltpu.VMEM((6, TP, 256), BF16),
             pltpu.VMEM((16, 16, TP), BF16),
+            pltpu.VMEM((32, 150), F32),
             pltpu.VMEM((8, 16, 150), F32),
             pltpu.VMEM((8, SURR, 75), jnp.int32),
             pltpu.VMEM((256, TP), F32),
@@ -402,7 +404,7 @@
             pltpu.VMEM((31, 1, 128), F32),
             pltpu.VMEM((1, 128), F32),
             pltpu.VMEM((15, 1, 128), F32),
-            dma((2,)), dma, dma, dma((2,)), dma, dma, dma, dma, dma, dma, dma((16,)),
+            dma((2,)), dma, dma, dma((2,)), dma, dma, dma, dma, dma, dma, dma((2,)), dma((4,)),
             dma, dma, dma, dma, dma, dma, dma, dma, pltpu.SemaphoreType.REGULAR,
         ],
         compiler_params=pltpu.CompilerParams(

time: 53.1 us -> 52.1 us (0.981)
  Pallas kernels: 51.3 us -> 50.2 us
    pallas_call x1, Pallas kernels: 51.3 us -> 50.2 us  [body(): pl.pallas_call(kernel, out_shape=(pltpu.VMEM((64, 128), F32), pltpu.VMEM(...]
where the time goes in v4:
time: 52.1 us; the launch traced here: 52 us
  Pallas kernels  50.2 us (96%)
  local copies, waits for them, and re-layouts  1.13 us (2%)
  between operations  0.64 us (1%)
    pallas_call x1, Pallas kernels, body(): pl.pallas_call(kernel, out_shape=(pltpu.VMEM((64, 128), F32), pltpu.VMEM(...  50.2 us

profile of v4, /device:TPU:1, one launch (start us, length us, event | category | flops | bytes accessed | tf_op | source)
XLA Modules:
  0.0 52.0 jit_solution(7719183617765320222)
XLA Ops:
  0.6 50.2 %surrogate_peaks.1 = (f32[64,128]{1,0:T(8,128)S(1)}, f32[1,128]{1,0:T(1,128)S(1)}) custom-call(bf16[1200,1536]{1,0:T(8,128)(2,1)} %series.1, f32[32,150]{1,0:T(8,128)} %bitcast.5, s32[4,75]{1,0:T(4,128)} %phase.1, f32[4,640,128]{2,1,0:T(8,128)} %constant.2.clone.basis), custom_call_target="tpu_custom_call" | custom-call | tf_op jit(solution)/shard_map/surrogate_peaks/pallas_call | solution.py:383
  50.9 0.6 %copy.8 = f32[4,2048,1]{1,2,0:T(1,128)} copy(f32[4,2048,1]{1,2,0:T(1,128)S(1)} %bitcast.4) | data formatting | bytes 65536
  51.5 0.5 slice_bitcast_fusion

commit v5 on v4

--- a/solution.py
+++ b/solution.py
@@ -24,8 +24,12 @@
 PLANE = tuple((dx, dk) for dx in (2, 1, 3, 0) for dk in (4, 5, 3, 2, 6, 7, 1, 0) if (dx, dk) != (0, 0))
 
 
+ORDER = np.concatenate([np.arange(2, 514, 2), np.arange(1, 513, 2), np.arange(514, 601, 2), np.arange(513, 600, 2)])
+LAST = 555
+
+
 def basis_tables():
-    freq = np.arange(1, FP + 1)[:, None]
+    freq = np.concatenate([ORDER, np.ones(FP - FREQS, ORDER.dtype)])[:, None]
     lane = np.arange(128)[None, :]
     fine = 2.0 * np.pi * ((freq * lane) % FRAMES) / FRAMES
     step = np.broadcast_to(2.0 * np.pi * ((freq * 128) % FRAMES) / FRAMES, fine.shape)
@@ -108,16 +112,17 @@
 
     def make_rows(i, _):
         at = pl.multiple_of(i * 64, 64)
+        sin_at = pl.multiple_of(FP + lax.rem(i + 2, 10) * 64, 64)
         c = bas[0, pl.ds(at, 64), :]
         s = bas[1, pl.ds(at, 64), :]
         sc = bas[2, pl.ds(at, 64), :]
         ss = bas[3, pl.ds(at, 64), :]
         for a in range(10):
             lanes = pl.ds(a * 128, 128)
-            for base, val in ((0, c), (FP, s)):
+            for rows, val in ((pl.ds(at, 64), c), (pl.ds(sin_at, 64), s)):
                 hi = val.astype(BF16)
-                thi[pl.ds(base + at, 64), lanes] = hi
-                tlo[pl.ds(base + at, 64), lanes] = (val - hi.astype(F32)).astype(BF16)
+                thi[rows, lanes] = hi
+                tlo[rows, lanes] = (val - hi.astype(F32)).astype(BF16)
             c, s = c * sc - s * ss, s * sc + c * ss
         return 0
 
@@ -186,9 +191,11 @@
     def _():
         chunks[k] = block_rows[pl.ds(pl.multiple_of(half * 16, 16), 16), :]
         await_all(chunks.at[pl.ds(0, 7)], chunk_recv)
-        x = jnp.concatenate([chunks[i] for i in range(8)], axis=1)
-        x = x - jnp.sum(x, axis=1, keepdims=True) * (1.0 / FRAMES)
-        held[xx] = jnp.concatenate([x, jnp.zeros((16, TP - FRAMES), F32)], axis=1).astype(BF16)
+        both = jnp.concatenate([chunks[i] + chunks[i + 4] for i in range(4)], axis=1)
+        apart = jnp.concatenate([chunks[i] - chunks[i + 4] for i in range(4)], axis=1)
+        both = both - jnp.sum(both, axis=1, keepdims=True) * (2.0 / FRAMES)
+        rest = jnp.zeros((16, FP - FREQS), F32)
+        held[xx] = jnp.concatenate([both, rest, apart, rest], axis=1).astype(BF16)
         send_own(NEAR)
 
     def arrived(rel):
@@ -272,44 +279,65 @@
 
     await_all(angles.at[pl.ds(0, 7)], ang_recv)
     turn = jnp.concatenate([angles[i] for i in range(8)] + [jnp.zeros((SURR, FP - FREQS), jnp.int32)], axis=1)
-    angle = turn.astype(F32) * (2.0 * math.pi / FRAMES)
+    digits = jnp.concatenate([lax.div(turn, 32), lax.rem(turn, 32)], axis=0).astype(F32).astype(BF16)
+    source = lax.broadcasted_iota(jnp.int32, (FP, FP), 0) + 1
+    place = lax.broadcasted_iota(jnp.int32, (FP, FP), 1)
+    freq = 2 * place + jnp.where(
+        place < 256, 2, jnp.where(place < 512, -511, jnp.where(place <= LAST, -510, jnp.where(place < FREQS, -599, FRAMES)))
+    )
+    moved = dot(digits, jnp.where(source == freq, 1.0, 0.0).astype(BF16))
+    angle = (moved[:SURR] * 32.0 + moved[SURR:]) * (2.0 * math.pi / FRAMES)
     lane = lax.broadcasted_iota(jnp.int32, (SURR, FP), 1)
-    weight = jnp.where(lane < FREQS - 1, 1.0, jnp.where(lane == FREQS - 1, 0.5, 0.0)).astype(F32)
+    weight = jnp.where(lane < FREQS, jnp.where(lane == LAST, 0.5, 1.0), 0.0).astype(F32)
     cos_phase = jnp.cos(angle) * weight
     sin_phase = jnp.sin(angle) * weight
     lane1 = lax.broadcasted_iota(jnp.int32, (1, FP), 1)
-    inner = (lane1 < FREQS - 1).astype(F32)
+    inner = ((lane1 < FREQS) & (lane1 != LAST)).astype(F32)
+    even_lane = lax.rem(lax.broadcasted_iota(jnp.int32, (128, 256), 1), 128) <= LAST - 512
     lane128 = lax.broadcasted_iota(jnp.int32, (256, 128), 1)
     row16 = lax.rem(lax.broadcasted_iota(jnp.int32, (256, 128), 0), 16)
 
     def spectra(h):
         await_all(held.at[pl.ds(0, 6)], x_recv.at[h])
-        xs = held[8 * h : 8 * h + 8].reshape(128, TP)
-        for j in range(5):
-            rows = pl.ds(j * 256, 256)
-            spec[pl.ds(128 * h, 128), rows] = dot_t(xs, thi[rows, :]) + dot_t(xs, tlo[rows, :])
+        rows = pl.ds(128 * h, 128)
+        both = held[8 * h : 8 * h + 8, :, 0:FP].reshape(128, FP)
+        apart = held[8 * h : 8 * h + 8, :, FP:TP].reshape(128, FP)
+
+        def spectrum(x, start):
+            table = pl.ds(start, 256)
+            return dot_t(x, thi[table, 0:FP]) + dot_t(x, tlo[table, 0:FP])
+
+        for start in (0, 768):
+            spec[rows, start : start + 256] = spectrum(both, start)
+            spec[rows, start + 256 : start + 512] = spectrum(apart, start + 256)
+        spec[rows, 512:768] = jnp.where(even_lane, spectrum(both, 512), spectrum(apart, 512))
+
+    def halves(rows):
+        sc = spec[rows, 0:FP]
+        ss = jnp.concatenate([spec[rows, 768:TP], spec[rows, FP:768]], axis=1)
+        return sc, ss
 
     def rotate(h, s):
-        sc = spec[pl.ds(128 * h, 128), 0:FP]
-        ss = spec[pl.ds(128 * h, 128), FP:TP]
+        sc, ss = halves(pl.ds(128 * h, 128))
         cp = cos_phase[s : s + 1, :]
         sp = sin_phase[s : s + 1, :]
         rows = pl.ds(s * 256 + 128 * h, 128)
         rot[rows, 0:FP] = (sc * cp + ss * sp).astype(BF16)
-        rot[rows, FP:TP] = (ss * cp - sc * sp).astype(BF16)
+        turned_back = (ss * cp - sc * sp).astype(BF16)
+        rot[rows, 768:TP] = turned_back[:, 0:512]
+        rot[rows, FP:768] = turned_back[:, 512:FP]
 
     spectra(0)
     for s in range(SURR):
         rotate(0, s)
     await_all(kc.at[pl.ds(0, 3)], kc_recv)
     spectra(1)
-    sc = spec[:, 0:FP]
-    ss = spec[:, FP:TP]
+    sc, ss = halves(pl.ds(0, 256))
     power = jnp.sum((sc * sc + ss * ss) * inner, axis=1, keepdims=True)
-    last = jnp.sum(jnp.where(lane1 == FREQS - 1, sc, 0.0), axis=1, keepdims=True)
+    last = jnp.sum(jnp.where(lane1 == LAST, sc, 0.0), axis=1, keepdims=True)
     scales = []
     for s in range(SURR):
-        end = 2.0 * cos_phase[s : s + 1, FREQS - 1 : FREQS] * last
+        end = 2.0 * cos_phase[s : s + 1, LAST : LAST + 1] * last
         energy = power * (2.0 / FRAMES) + end * end * (1.0 / FRAMES)
         scales.append(lax.rsqrt(energy + EPS) * (math.sqrt(FRAMES) * 2.0 / FRAMES))
     for s in range(SURR):

time: 52.1 us -> 51 us (0.979)
  Pallas kernels: 50.2 us -> 49.1 us
    pallas_call x1, Pallas kernels: 50.2 us -> 49.1 us  [body(): pl.pallas_call(kernel, out_shape=(pltpu.VMEM((64, 128), F32), pltpu.VMEM(...]
where the time goes in v5:
time: 51 us; the launch traced here: 50.9 us
  Pallas kernels  49.1 us (96%)
  local copies, waits for them, and re-layouts  1.13 us (2%)
  between operations  0.64 us (1%)
    pallas_call x1, Pallas kernels, body(): pl.pallas_call(kernel, out_shape=(pltpu.VMEM((64, 128), F32), pltpu.VMEM(...  49.1 us

profile of v5, /device:TPU:1, one launch (start us, length us, event | category | flops | bytes accessed | tf_op | source)
XLA Modules:
  0.0 50.9 jit_solution(12496338733171102694)
XLA Ops:
  0.6 49.1 %surrogate_peaks.1 = (f32[64,128]{1,0:T(8,128)S(1)}, f32[1,128]{1,0:T(1,128)S(1)}) custom-call(bf16[1200,1536]{1,0:T(8,128)(2,1)} %series.1, f32[32,150]{1,0:T(8,128)} %bitcast.5, s32[4,75]{1,0:T(4,128)} %phase.1, f32[4,640,128]{2,1,0:T(8,128)} %constant.2.clone.basis), custom_call_target="tpu_custom_call" | custom-call | tf_op jit(solution)/shard_map/surrogate_peaks/pallas_call | solution.py:411
  49.7 0.6 %copy.8 = f32[4,2048,1]{1,2,0:T(1,128)} copy(f32[4,2048,1]{1,2,0:T(1,128)S(1)} %bitcast.4) | data formatting | bytes 65536
  50.4 0.5 %slice_bitcast_fusion = f32[4]{0:T(128)} fusion(f32[1,128]{1,0:T(1,128)S(1)} %get-tuple-element.5), kind=kLoop, calls=%fused_computation | loop fusion | bytes 32 | tf_op jit(solution)/shard_map/squeeze | solution.py:443

commit v6 on v5

--- a/solution.py
+++ b/solution.py
@@ -46,7 +46,7 @@
 
 def kernel(
     series, slab, phase, basis, out_tile, out_peak,
-    cols, bas, thi, tlo, kc, held, block_rows, chunks, angles, spec, rot, best, mine, parts, own_top, top1, wide_top, top2,
+    cols, bas, thi, tlo, kc, held, block_rows, chunks, angles, spec, rot, mine, parts, own_top, top1, wide_top, top2,
     own_sem, col_sem, bas_sem, chunk_send, chunk_recv, ang_send, ang_recv, near_send, relay_send, x_send, x_recv, unit_recv,
     kc_send, kc_recv, part_send, part_recv, t1_send, t1_recv, t2_send, t2_recv, hello,
 ):
@@ -317,6 +317,11 @@
         ss = jnp.concatenate([spec[rows, 768:TP], spec[rows, FP:768]], axis=1)
         return sc, ss
 
+    def power(h):
+        sc, ss = halves(pl.ds(128 * h, 128))
+        inside = jnp.sum((sc * sc + ss * ss) * inner, axis=1, keepdims=True)
+        return inside, jnp.sum(jnp.where(lane1 == LAST, sc, 0.0), axis=1, keepdims=True)
+
     def rotate(h, s):
         sc, ss = halves(pl.ds(128 * h, 128))
         cp = cos_phase[s : s + 1, :]
@@ -328,29 +333,28 @@
         rot[rows, FP:768] = turned_back[:, 512:FP]
 
     spectra(0)
+    powers = [power(0)]
     for s in range(SURR):
         rotate(0, s)
     await_all(kc.at[pl.ds(0, 3)], kc_recv)
     spectra(1)
-    sc, ss = halves(pl.ds(0, 256))
-    power = jnp.sum((sc * sc + ss * ss) * inner, axis=1, keepdims=True)
-    last = jnp.sum(jnp.where(lane1 == LAST, sc, 0.0), axis=1, keepdims=True)
+    powers.append(power(1))
     scales = []
     for s in range(SURR):
-        end = 2.0 * cos_phase[s : s + 1, LAST : LAST + 1] * last
-        energy = power * (2.0 / FRAMES) + end * end * (1.0 / FRAMES)
-        scales.append(lax.rsqrt(energy + EPS) * (math.sqrt(FRAMES) * 2.0 / FRAMES))
+        energy = []
+        for inside, last in powers:
+            end = 2.0 * cos_phase[s : s + 1, LAST : LAST + 1] * last
+            energy.append(inside * (2.0 / FRAMES) + end * end * (1.0 / FRAMES))
+        scales.append(lax.rsqrt(jnp.concatenate(energy, axis=0) + EPS) * (math.sqrt(FRAMES) * 2.0 / FRAMES))
+    placed = jnp.zeros((256, 128), F32)
     for s in range(SURR):
         rotate(1, s)
         rows = pl.ds(s * 256, 256)
         for j in range(6):
             score = jnp.abs(dot(rot[rows, :], kc[j]))
             score = jnp.maximum(score[:, :128], score[:, 128:])
-            best[rows, :] = score if j == 0 else jnp.maximum(best[rows, :], score)
-    placed = jnp.zeros((256, 128), F32)
-    for s in range(SURR):
-        top = jnp.max(best[pl.ds(s * 256, 256), :], axis=1, keepdims=True) * scales[s]
-        placed = jnp.where(lane128 == row16 + 16 * s, top, placed)
+            tops = score if j == 0 else jnp.maximum(tops, score)
+        placed = jnp.where(lane128 == row16 + 16 * s, jnp.max(tops, axis=1, keepdims=True) * scales[s], placed)
     found = jnp.max(placed.reshape(16, 16, 128), axis=1)
     for n in range(16):
         row = (n % 4) * 4 + lax.rem(behind + n // 4, 4)
@@ -425,7 +429,6 @@
             pltpu.VMEM((8, SURR, 75), jnp.int32),
             pltpu.VMEM((256, TP), F32),
             pltpu.VMEM((1024, TP), BF16),
-            pltpu.VMEM((1024, 128), F32),
             pltpu.VMEM((16, 128), F32),
             pltpu.VMEM((8, 16, 128), F32),
             pltpu.VMEM((1, 128), F32),

time: 51 us -> 51 us (level)
  no operation moved by 1% of the time
where the time goes in v6:
time: 51 us; the launch traced here: 50.9 us
  Pallas kernels  49.1 us (96%)
  local copies, waits for them, and re-layouts  1.13 us (2%)
  between operations  0.64 us (1%)
    pallas_call x1, Pallas kernels, body(): pl.pallas_call(kernel, out_shape=(pltpu.VMEM((64, 128), F32), pltpu.VMEM(...  49.1 us

profile of v6, /device:TPU:1, one launch (start us, length us, event | category | flops | bytes accessed | tf_op | source)
XLA Modules:
  0.0 50.9 jit_solution(17821843487899942618)
XLA Ops:
  0.6 49.1 %surrogate_peaks.1 = (f32[64,128]{1,0:T(8,128)S(1)}, f32[1,128]{1,0:T(1,128)S(1)}) custom-call(bf16[1200,1536]{1,0:T(8,128)(2,1)} %series.1, f32[32,150]{1,0:T(8,128)} %bitcast.5, s32[4,75]{1,0:T(4,128)} %phase.1, f32[4,640,128]{2,1,0:T(8,128)} %constant.2.clone.basis), custom_call_target="tpu_custom_call" | custom-call | tf_op jit(solution)/shard_map/surrogate_peaks/pallas_call | solution.py:415
  49.7 0.6 %copy.8 = f32[4,2048,1]{1,2,0:T(1,128)} copy(f32[4,2048,1]{1,2,0:T(1,128)S(1)} %bitcast.4) | data formatting | bytes 65536
  50.4 0.5 %slice_bitcast_fusion = f32[4]{0:T(128)} fusion(f32[1,128]{1,0:T(1,128)S(1)} %get-tuple-element.5), kind=kLoop, calls=%fused_computation | loop fusion | bytes 32 | tf_op jit(solution)/shard_map/squeeze | solution.py:446

commit v7 on v6

--- a/solution.py
+++ b/solution.py
@@ -356,20 +356,19 @@
             tops = score if j == 0 else jnp.maximum(tops, score)
         placed = jnp.where(lane128 == row16 + 16 * s, jnp.max(tops, axis=1, keepdims=True) * scales[s], placed)
     found = jnp.max(placed.reshape(16, 16, 128), axis=1)
+    own_top[...] = jnp.max(found, axis=0, keepdims=True)
+    for n, (dx, dk) in enumerate(PLANE):
+        remote(own_top, top1.at[n], t1_send, t1_recv, at_xk(dx, dk)).start()
     for n in range(16):
         row = (n % 4) * 4 + lax.rem(behind + n // 4, 4)
         mine[pl.ds(row, 1), :] = found[n : n + 1, :]
-
-    own_top[...] = jnp.max(mine[...], axis=0, keepdims=True)
-    for n, (dx, dk) in enumerate(PLANE):
-        remote(own_top, top1.at[n], t1_send, t1_recv, at_xk(dx, dk)).start()
-    for d in range(1, 8):
-        remote(mine, parts.at[k], part_send, part_recv, at_k(d)).start()
-    parts[k] = mine[...]
     await_all(top1, t1_recv)
     wide_top[...] = jnp.maximum(own_top[...], jnp.max(top1[...], axis=0))
     for n, d in enumerate(RING):
         remote(wide_top, top2.at[n], t2_send, t2_recv, at_z(d)).start()
+    for d in range(1, 8):
+        remote(mine, parts.at[k], part_send, part_recv, at_k(d)).start()
+    parts[k] = mine[...]
     await_all(parts.at[pl.ds(0, 7)], part_recv)
     lane16 = lax.broadcasted_iota(jnp.int32, (16, 128), 1)
     for s in range(SURR):

time: 51 us -> 51 us (level)
  no operation moved by 1% of the time
where the time goes in v7:
time: 51 us; the launch traced here: 50.9 us
  Pallas kernels  49.1 us (96%)
  local copies, waits for them, and re-layouts  1.13 us (2%)
  between operations  0.64 us (1%)
    pallas_call x1, Pallas kernels, body(): pl.pallas_call(kernel, out_shape=(pltpu.VMEM((64, 128), F32), pltpu.VMEM(...  49.1 us

profile of v7, /device:TPU:1, one launch (start us, length us, event | category | flops | bytes accessed | tf_op | source)
XLA Modules:
  0.0 50.9 jit_solution(4899374261959187539)
XLA Ops:
  0.6 49.1 %surrogate_peaks.1 = (f32[64,128]{1,0:T(8,128)S(1)}, f32[1,128]{1,0:T(1,128)S(1)}) custom-call(bf16[1200,1536]{1,0:T(8,128)(2,1)} %series.1, f32[32,150]{1,0:T(8,128)} %bitcast.5, s32[4,75]{1,0:T(4,128)} %phase.1, f32[4,640,128]{2,1,0:T(8,128)} %constant.2.clone.basis), custom_call_target="tpu_custom_call" | custom-call | tf_op jit(solution)/shard_map/surrogate_peaks/pallas_call | solution.py:414
  49.7 0.6 %copy.8 = f32[4,2048,1]{1,2,0:T(1,128)} copy(f32[4,2048,1]{1,2,0:T(1,128)S(1)} %bitcast.4) | data formatting | bytes 65536
  50.3 0.5 %slice_bitcast_fusion = f32[4]{0:T(128)} fusion(f32[1,128]{1,0:T(1,128)S(1)} %get-tuple-element.5), kind=kLoop, calls=%fused_computation | loop fusion | bytes 32 | tf_op jit(solution)/shard_map/squeeze | solution.py:445

commit v8 on v6

--- a/solution.py
+++ b/solution.py
@@ -347,14 +347,17 @@
             energy.append(inside * (2.0 / FRAMES) + end * end * (1.0 / FRAMES))
         scales.append(lax.rsqrt(jnp.concatenate(energy, axis=0) + EPS) * (math.sqrt(FRAMES) * 2.0 / FRAMES))
     placed = jnp.zeros((256, 128), F32)
-    for s in range(SURR):
-        rotate(1, s)
-        rows = pl.ds(s * 256, 256)
+    for pair in range(2):
+        for s in (2 * pair, 2 * pair + 1):
+            rotate(1, s)
+        rows = pl.ds(pair * 512, 512)
         for j in range(6):
             score = jnp.abs(dot(rot[rows, :], kc[j]))
             score = jnp.maximum(score[:, :128], score[:, 128:])
             tops = score if j == 0 else jnp.maximum(tops, score)
-        placed = jnp.where(lane128 == row16 + 16 * s, jnp.max(tops, axis=1, keepdims=True) * scales[s], placed)
+        for s in (2 * pair, 2 * pair + 1):
+            own = tops[256 * (s % 2) : 256 * (s % 2) + 256]
+            placed = jnp.where(lane128 == row16 + 16 * s, jnp.max(own, axis=1, keepdims=True) * scales[s], placed)
     found = jnp.max(placed.reshape(16, 16, 128), axis=1)
     for n in range(16):
         row = (n % 4) * 4 + lax.rem(behind + n // 4, 4)

time: 51 us -> 51.3 us (level)
  no operation moved by 1% of the time
where the time goes in v8:
time: 51.3 us; the launch traced here: 51.2 us
  Pallas kernels  49.4 us (96%)
  local copies, waits for them, and re-layouts  1.13 us (2%)
  between operations  0.64 us (1%)
    pallas_call x1, Pallas kernels, body(): pl.pallas_call(kernel, out_shape=(pltpu.VMEM((64, 128), F32), pltpu.VMEM(...  49.4 us

profile of v8, /device:TPU:1, one launch (start us, length us, event | category | flops | bytes accessed | tf_op | source)
XLA Modules:
  0.0 51.2 jit_solution(563333318117068754)
XLA Ops:
  0.6 49.4 %surrogate_peaks.1 = (f32[64,128]{1,0:T(8,128)S(1)}, f32[1,128]{1,0:T(1,128)S(1)}) custom-call(bf16[1200,1536]{1,0:T(8,128)(2,1)} %series.1, f32[32,150]{1,0:T(8,128)} %bitcast.5, s32[4,75]{1,0:T(4,128)} %phase.1, f32[4,640,128]{2,1,0:T(8,128)} %constant.2.clone.basis), custom_call_target="tpu_custom_call" | custom-call | tf_op jit(solution)/shard_map/surrogate_peaks/pallas_call | solution.py:418
  50.0 0.6 %copy.8 = f32[4,2048,1]{1,2,0:T(1,128)} copy(f32[4,2048,1]{1,2,0:T(1,128)S(1)} %bitcast.4) | data formatting | bytes 65536
  50.7 0.5 slice_bitcast_fusion
